TPU v7x, 512 devices: a whole 4x4x16 slice. The times are simulated.
512 devices in a mesh: row: 16 (over y, x), col: 16 (over z), depth: 2 (over core).
Axes of the slice: x: 4, y: 4, z: 16, core: 2. Of those that a mesh axis runs over, the one named last changes fastest.
Arguments:
- features: bfloat16 [2, 16384, 1024], P('depth', ('row', 'col')), may hold values from -1.0546875 to 1.0546875
Outputs:
- drift: float32 [16384, 16384], P(('row', 'depth'), 'col')
All inputs are finite; a program needn't handle non-finite values.
Results may differ from a plain program's by a relative error of at most 0.0003.
Values may be sent and summed in bfloat16 or wider, within the bound.
No kernel may reach another device: no remote copies, remote signals or barrier semaphores. Data moves between devices by JAX's collectives and lax.ppermute only.
A program may use at most 64 MiB of HBM per device.

v0:
```python
import jax
import jax.numpy as jnp
from jax import lax
from jax.sharding import PartitionSpec as P


def broadcast(value, axis, source):
    kept = jnp.where(lax.axis_index(axis) == source, value, 0).astype(value.dtype)
    return lax.psum(kept, axis)


def transposed_product(left_rows, right_rows):
    return lax.dot_general(
        left_rows, right_rows, (((1,), (1,)), ((), ())), preferred_element_type=jnp.float32
    )


def body(features):
    rows_of = lax.axis_size("row")
    cols_of = lax.axis_size("col")
    own_shard = features[0]
    ex_dev = own_shard.shape[0]
    feat_width = own_shard.shape[1]
    per_dest = ex_dev // cols_of
    grouped = own_shard.reshape(cols_of, per_dest, 1, feat_width)
    row_piece = lax.all_to_all(grouped, "col", split_axis=0, concat_axis=2, tiled=True)
    row_block = lax.all_gather(row_piece.reshape(ex_dev, feat_width), "col", axis=0, tiled=True)
    col_ratio = cols_of // rows_of
    col_index = lax.axis_index("col")
    col_block = broadcast(row_block, "row", col_index // col_ratio)
    depth_index = lax.axis_index("depth")
    signum = 2.0 * depth_index.astype(jnp.float32) - 1.0
    return lax.psum_scatter(
        signum * transposed_product(row_block, col_block), "depth", scatter_dimension=0, tiled=True
    )


def solution(mesh):
    placed = (P("depth", ("row", "col"), None),)
    return jax.shard_map(
        body, mesh=mesh, in_specs=placed, out_specs=P(("row", "depth"), "col"), check_vma=False
    )
```

profile of v0, /device:TPU:1, one launch (start us, length us, event | category | flops | bytes accessed | tf_op | source)
XLA Modules:
  0.0 265.4 jit_solution(9115069896049042623)
XLA Ops:
  6.5 0.0 all-gather.2.cloned.1.call-start
  6.5 1.0 reshape_squeeze.3
  7.5 27.5 %all_to_all.15 = bf16[16,4,1,1024]{3,1,2,0:T(4,128)(2,1)S(1)} all-to-all(bf16[16,4,1,1024]{3,1,2,0:T(4,128)(2,1)S(1)} %bitcast.11), channel_id=1, replica_groups=mesh['row'=16,'col'=16,'depth'=2] {'col'}, dimensions={0} | all-to-all | bytes 262144 | tf_op jit(solution)/shard_map/all_to_all | solution.py:26
  35.0 0.7 copy.7
  35.7 0.0 all-gather.2.cloned.1.call-update
  35.8 0.0 all-reduce.2.cloned.1.call-start
  35.8 60.2 %all-gather.2.cloned.1.call-done = bf16[1024,1024]{1,0:T(8,128)(2,1)} async-done(((bf16[64,1024]{1,0:T(8,128)(2,1)}), bf16[1024,1024]{1,0:T(8,128)(2,1)}) %all-gather.2.cloned.1.call-update) | async-done | bytes 2097168 | tf_op jit(solution)/shard_map/all_gather | solution.py:27
  96.1 3.0 %broadcast_select_fusion = bf16[1024,1024]{1,0:T(8,128)(2,1)} fusion(bf16[1024,1024]{1,0:T(8,128)(2,1)} %all-gather.2.cloned.1.call-done, pred[]{:T(512)S(6)} %eq.3), kind=kLoop, calls=%fused_computation.1 | loop fusion | flops 1048576 | bytes 4194305 | tf_op jit(solution)/shard_map/jit(_where)/select_n | solution.py:8
  99.1 0.0 copy-start
  99.1 0.0 all-reduce.2.cloned.1.call-update
  99.1 0.0 reduce-scatter.2.cloned.1.call-start
  99.2 126.3 %all-reduce.2.cloned.1.call-done = bf16[1024,1024]{1,0:T(8,128)(2,1)} async-done(((bf16[1024,1024]{1,0:T(8,128)(2,1)}), bf16[1024,1024]{1,0:T(8,128)(2,1)}) %all-reduce.2.cloned.1.call-update) | async-done | bytes 2097168 | tf_op jit(solution)/shard_map/psum | solution.py:9
  225.5 0.0 copy-done
  225.5 5.9 %multiply_bitcast_fusion = f32[1024,1024]{0,1:T(8,128)} fusion(bf16[1024,1024]{1,0:T(8,128)(2,1)} %all-reduce.2.cloned.1.call-done, bf16[1024,1024]{1,0:T(8,128)(2,1)S(1)} %copy-done, f32[]{:T(128)S(6)} %sub.5), kind=kOutput, calls=%fused_computation | convolution fusion | flops 2148532224 | bytes 8388612 | tf_op jit(solution)/shard_map/dot_general | solution.py:13
  231.4 0.0 reduce-scatter.2.cloned.1.call-update
  231.4 24.6 %reduce-scatter.2.cloned.1.call-done = f32[512,1024]{0,1:T(8,128)} async-done(((f32[1024,1024]{0,1:T(8,128)}), f32[512,1024]{0,1:T(8,128)}) %reduce-scatter.2.cloned.1.call-update) | async-done | bytes 2097168 | tf_op jit(solution)/shard_map/reduce_scatter | solution.py:33
  256.0 2.9 %copy.8 = f32[512,1024]{1,0:T(8,128)} copy(f32[512,1024]{0,1:T(8,128)} %reduce-scatter.2.cloned.1.call-done) | data formatting | bytes 4194304 | tf_op jit(solution)/shard_map/reduce_scatter | solution.py:33
Async XLA Ops:
  6.5 89.5 %all-gather.2.cloned.1.call-start = ((), (), s32[]{:S(2)}) async-start(), calls=%async_computation.2 | async-start | bytes 2228224 | tf_op jit(solution)/shard_map/all_gather | solution.py:27
  35.8 189.7 %all-reduce.2.cloned.1.call-start = ((), (), s32[]{:S(2)}) async-start(), calls=%async_computation.3 | async-start | bytes 4194304 | tf_op jit(solution)/shard_map/psum | solution.py:9
  99.1 126.4 %copy-start = (bf16[1024,1024]{1,0:T(8,128)(2,1)S(1)}, bf16[1024,1024]{1,0:T(8,128)(2,1)}, u32[]{:S(2)}) copy-start(bf16[1024,1024]{1,0:T(8,128)(2,1)} %all-gather.2.cloned.1.call-done) | copy-start | bytes 6291460
  99.1 156.8 %reduce-scatter.2.cloned.1.call-start = ((), (), s32[]{:S(2)}) async-start(), calls=%async_computation.4 | async-start | bytes 6291456 | tf_op jit(solution)/shard_map/reduce_scatter | solution.py:33
Sparse Core Ops, SparseCore 0:
  35.9 60.1 all-gather.1
  99.4 126.0 all-reduce.1
  231.5 24.4 reduce-scatter.1
where the time goes:
time: 266 us; the launch traced here: 265 us
  waiting for transfers between devices  211 us (79%)
  blocking collectives  27.5 us (10%)
  between operations  13.1 us (5%)
  matrix products  5.9 us (2%)
  local copies, waits for them, and re-layouts  4.54 us (2%)
  other arithmetic  3.05 us (1%)
    psum x1, waiting for transfers between devices, broadcast(): return lax.psum(kept, axis)  126 us
    all_gather x1, waiting for transfers between devices, body(): lax.all_gather(row_piece.reshape(ex_dev, feat_width), 'col', axis=0, tile...  60.2 us
    all_to_all x1, blocking collectives, body(): lax.all_to_all(grouped, 'col', split_axis=0, concat_axis=2, tiled=True)  27.5 us
    reduce_scatter x1, waiting for transfers between devices, body(): lax.psum_scatter(signum * transposed_product(row_block, col_block), 'dept...  24.6 us
    dot_general x1, matrix products, transposed_product(): lax.dot_general(left_rows, right_rows, (((1,), (1,)), ((), ())), preferre...  5.9 us
  transfers between devices with their start and end apart: 3, of which 3 were waited for; matrix products, arithmetic and copies ran while one was open for 0% of the time, Pallas kernels for 0%

commit v1 on v0

v1 whole, which is shorter than its diff:
```python
import jax
import jax.numpy as jnp
from jax import lax
from jax.experimental import pallas as pl
from jax.experimental.pallas import tpu as pltpu
from jax.sharding import PartitionSpec as P

STRIDE = 4


def order_rows(place_ref, group_refs, rows_ref, half):
    piece_rows = rows_ref.shape[0] // sum(ref.shape[0] for ref, _, _ in group_refs)
    start = pl.multiple_of(half * piece_rows, piece_rows)
    for ref, offset, first in group_refs:
        residue = lax.rem(place_ref[0] + offset, STRIDE)
        for g in range(ref.shape[0]):
            piece = residue + STRIDE * (first + g)
            rows_ref[pl.ds(pl.multiple_of(piece * piece_rows, piece_rows), piece_rows), :] = ref[
                g, pl.ds(start, piece_rows), :
            ]


def interleave(pieces):
    count, rows, width = pieces.shape
    return pieces.transpose(1, 0, 2).reshape(count * rows, width)


def half_product(place_ref, rows, cols, pieces):
    tile = lax.dot_general(
        rows, cols, (((1,), (1,)), ((), ())), preferred_element_type=jnp.float32
    )
    tile = tile * (2 * place_ref[1] - 1).astype(jnp.float32)
    return interleave(tile.reshape(pieces, tile.shape[0] // pieces, tile.shape[1]))


def groups_of(own_ref, before_ref, after_ref, low_ref, high_ref):
    return (
        (own_ref, 0, 0),
        (before_ref, STRIDE - 1, 0),
        (after_ref, 1, 0),
        (low_ref, 2, 0),
        (high_ref, 2, low_ref.shape[0]),
    )


def send_kernel(
    place_ref, own_ref, before_ref, after_ref, low_ref, high_ref, raw_ref,
    out_ref, cols_ref, rows_scr, turned_scr,
):
    pieces = raw_ref.shape[0]
    for j in range(pieces):
        turned_scr[j] = raw_ref[lax.rem(place_ref[0] + j, pieces)]

    @pl.when(pl.program_id(0) == 0)
    def _():
        groups = groups_of(own_ref, before_ref, after_ref, low_ref, high_ref)
        order_rows(place_ref, groups, rows_scr, 1 - place_ref[1])

    cols = interleave(turned_scr[...])
    cols_ref[...] = cols
    out_ref[...] = half_product(place_ref, rows_scr[...], cols, raw_ref.shape[0])


def keep_kernel(
    place_ref, own_ref, before_ref, after_ref, low_ref, high_ref, cols_ref, out_ref, rows_scr,
):
    @pl.when(pl.program_id(0) == 0)
    def _():
        groups = groups_of(own_ref, before_ref, after_ref, low_ref, high_ref)
        order_rows(place_ref, groups, rows_scr, place_ref[1])

    pieces = rows_scr.shape[0] * 2 // own_ref.shape[1]
    out_ref[...] = half_product(place_ref, rows_scr[...], cols_ref[...], pieces)


def partial_products(place, groups, raw):
    pieces, ex_dev, feat_width = raw.shape
    width = pieces * ex_dev
    half = width // 2
    steps = 2
    tile = width // steps
    whole = [pl.BlockSpec(g.shape, lambda n, p: (0, 0, 0)) for g in groups]
    params = pltpu.CompilerParams(
        dimension_semantics=("arbitrary",), vmem_limit_bytes=48 << 20
    )
    out_spec = pl.BlockSpec((half, tile), lambda n, p: (0, n))
    cols_spec = pl.BlockSpec((tile, feat_width), lambda n, p: (n, 0))
    rows_scr = pltpu.VMEM((half, feat_width), jnp.bfloat16)
    sent, cols = pl.pallas_call(
        send_kernel,
        out_shape=(
            jax.ShapeDtypeStruct((half, width), jnp.float32),
            jax.ShapeDtypeStruct((width, feat_width), jnp.bfloat16),
        ),
        grid_spec=pltpu.PrefetchScalarGridSpec(
            num_scalar_prefetch=1,
            grid=(steps,),
            in_specs=whole
            + [pl.BlockSpec((pieces, ex_dev // steps, feat_width), lambda n, p: (0, n, 0))],
            out_specs=(out_spec, cols_spec),
            scratch_shapes=[
                rows_scr,
                pltpu.VMEM((pieces, ex_dev // steps, feat_width), jnp.bfloat16),
            ],
        ),
        compiler_params=params,
    )(place, *groups, raw)
    kept = pl.pallas_call(
        keep_kernel,
        out_shape=jax.ShapeDtypeStruct((half, width), jnp.float32),
        grid_spec=pltpu.PrefetchScalarGridSpec(
            num_scalar_prefetch=1,
            grid=(steps,),
            in_specs=whole + [cols_spec],
            out_specs=out_spec,
            scratch_shapes=[rows_scr],
        ),
        compiler_params=params,
    )(place, *groups, cols)
    return sent, kept


def body(features):
    rows_of = lax.axis_size("row")
    cols_of = lax.axis_size("col")
    own = features[0]
    ex_dev, feat_width = own.shape
    col = lax.axis_index("col").astype(jnp.int32)
    depth = lax.axis_index("depth").astype(jnp.int32)
    members = cols_of // STRIDE

    def shifted(value, by):
        return lax.ppermute(value, "col", [(z, (z + by) % cols_of) for z in range(cols_of)])

    grid = [(r, c) for r in range(rows_of) for c in range(cols_of)]
    spread = [(r * cols_of + c, ((r + c) % rows_of) * cols_of + c) for r, c in grid]
    mirror = [(q * cols_of + c, q * cols_of + (q - c) % cols_of) for q, c in grid]
    strided = [[z + STRIDE * g for g in range(members)] for z in range(STRIDE)]

    piece = lax.ppermute(own, ("row", "col"), spread)
    held = lax.all_gather(own, "col", axis=0, tiled=False, axis_index_groups=strided)
    piece, held = lax.optimization_barrier((piece, held))
    piece = lax.ppermute(piece, ("row", "col"), mirror)

    copies = jnp.broadcast_to(piece[None], (rows_of, ex_dev, feat_width))
    raw = lax.all_to_all(copies, "row", split_axis=0, concat_axis=0, tiled=True)

    before = shifted(held, 1)
    after = shifted(held, -1)
    low = shifted(held[: members // 2], 2)
    high = shifted(held[members // 2 :], -2)

    groups = (held, before, after, low, high)
    sent, kept = partial_products(jnp.stack([col, depth]), groups, raw)
    return kept + lax.ppermute(sent, "depth", [(0, 1), (1, 0)])


def solution(mesh):
    placed = (P("depth", ("row", "col"), None),)
    return jax.shard_map(
        body, mesh=mesh, in_specs=placed, out_specs=P(("row", "depth"), "col"), check_vma=False
    )
```

time: 266 us -> 106 us (0.40)
  waiting for transfers between devices: 211 us -> 13.8 us
  starting transfers between devices: 0.09 us -> 49.1 us
  between operations: 13.1 us -> 0.11 us
  Pallas kernels: 0 us -> 8.67 us
  matrix products: 5.9 us -> 0 us
  blocking collectives: 27.5 us -> 30.5 us
  local copies, waits for them, and re-layouts: 4.54 us -> 1.62 us
    psum x1 -> x0, waiting for transfers between devices: 126 us -> none  [broadcast(): return lax.psum(kept, axis)]
    all_gather x1 -> x0, waiting for transfers between devices: 60.2 us -> none  [body(): lax.all_gather(row_piece.reshape(ex_dev, feat_width), 'col', axis=0, tile...]
    all_gather x0 -> x1, blocking collectives: none -> 30.5 us  [body(): lax.all_gather(own, 'col', axis=0, tiled=False, axis_index_groups=strided)]
    all_to_all x1 -> x0, blocking collectives: 27.5 us -> none  [body(): lax.all_to_all(grouped, 'col', split_axis=0, concat_axis=2, tiled=True)]
    ppermute x0 -> x7, starting transfers between devices: none -> 24.6 us  [the longest x4 15.2 us: shifted(): lax.ppermute(value, 'col', [(z, (z + by) % cols_of) for z in range(cols_o...]
    reduce_scatter x1 -> x0, waiting for transfers between devices: 24.6 us -> none  [body(): lax.psum_scatter(signum * transposed_product(row_block, col_block), 'dept...]
    all_to_all x0 -> x1, starting transfers between devices: none -> 24.5 us  [body(): raw = lax.all_to_all(copies, 'row', split_axis=0, concat_axis=0, tiled=True)]
    ppermute x0 -> x7, waiting for transfers between devices: none -> 13.8 us  [the longest x4 13.8 us: shifted(): lax.ppermute(value, 'col', [(z, (z + by) % cols_of) for z in range(cols_o...]
  transfers between devices with their start and end apart: 3 -> 8, of which waited for: 3 -> 1; matrix products, arithmetic and copies ran while one was open for 0% -> 0% of each run, Pallas kernels for 0% -> 4%
where the time goes in v1:
time: 106 us
  starting transfers between devices  49.1 us (46%)
  blocking collectives  30.5 us (29%)
  waiting for transfers between devices  13.8 us (13%)
  Pallas kernels  8.67 us (8%)
  other arithmetic  1.82 us (2%)
  local copies, waits for them, and re-layouts  1.62 us (2%)
    all_gather x1, blocking collectives, body(): lax.all_gather(own, 'col', axis=0, tiled=False, axis_index_groups=strided)  30.5 us
    all_to_all x1, starting transfers between devices, body(): raw = lax.all_to_all(copies, 'row', split_axis=0, concat_axis=0, tiled=True)  24.5 us
    ppermute x4, starting transfers between devices, shifted(): lax.ppermute(value, 'col', [(z, (z + by) % cols_of) for z in range(cols_o...  15.2 us
    ppermute x4, waiting for transfers between devices, shifted(): lax.ppermute(value, 'col', [(z, (z + by) % cols_of) for z in range(cols_o...  13.8 us
    ppermute x1, starting transfers between devices, body(): return kept + lax.ppermute(sent, 'depth', [(0, 1), (1, 0)])  7.2 us
    pallas_call x1, Pallas kernels, partial_products(): pl.pallas_call(send_kernel, out_shape=(jax.ShapeDtypeStruct((half, width)...  4.92 us
    pallas_call x1, Pallas kernels, partial_products(): pl.pallas_call(keep_kernel, out_shape=jax.ShapeDtypeStruct((half, width),...  3.75 us
  transfers between devices with their start and end apart: 8, of which 1 were waited for; matrix products, arithmetic and copies ran while one was open for 0% of the time, Pallas kernels for 4%

profile of v1, /device:TPU:1, one launch (start us, length us, event | category | flops | bytes accessed | tf_op | source)
XLA Modules:
  0.0 105.5 jit_solution(1342483854211085526)
XLA Ops:
  0.0 1.6 %collective-permute-start = (bf16[64,1024]{1,0:T(8,128)(2,1)}, bf16[64,1024]{1,0:T(8,128)(2,1)S(1)}, u32[]{:S(2)}, u32[]{:S(2)}) collective-permute-start(bf16[64,1024]{1,0:T(8,128)(2,1)} %bitcast.3), channel_id=1, source_target_pairs={{0,0},{2,34},{4,68},{6,102},{8,136},{10,170},{12,204},{14,238},{16... | collective-permute-start | bytes 393224 | tf_op jit(solution)/shard_map/ppermute | solution.py:140
  1.6 30.5 %all_gather.3.own_ref = bf16[4,64,1024]{2,1,0:T(8,128)(2,1)S(1)} all-gather(bf16[1,64,1024]{2,1,0:T(8,128)(2,1)} %param.1), channel_id=1, replica_groups={{0,8,16,24},{2,10,18,26},{4,12,20,28},{6,14,22,30},{1,9,17,25},{3,11,19..., dimensions={0}, use_global_device_ids=true | all-gather | bytes 655360 | tf_op jit(solution)/shard_map/all_gather | solution.py:141
  32.0 0.0 collective-permute-done
  32.0 0.7 collective-permute-start.5
  32.7 0.0 collective-permute-done.5
  32.7 1.6 %broadcast_in_dim.2 = bf16[16,64,1024]{2,1,0:T(8,128)(2,1)} broadcast(bf16[64,1024]{1,0:T(8,128)(2,1)S(1)} %collective-permute-done.5), dimensions={1,2} | broadcast | bytes 2228224 | tf_op jit(solution)/shard_map/broadcast_in_dim | solution.py:145
  34.3 24.5 %all-to-all-start = ((bf16[16,64,1024]{2,1,0:T(8,128)(2,1)}), bf16[16,64,1024]{2,1,0:T(8,128)(2,1)}, u32[]{:S(2)}, u32[]{:S(2)}) async-start(bf16[16,64,1024]{2,1,0:T(8,128)(2,1)} %broadcast_in_dim.2), calls=%async_computation | async-start | bytes 4194304 | tf_op jit(solution)/shard_map/all_to_all | solution.py:146
  58.8 7.1 %collective-permute-start.2 = (bf16[4,64,1024]{2,1,0:T(8,128)(2,1)S(1)}, bf16[4,64,1024]{2,1,0:T(8,128)(2,1)S(1)}, u32[]{:S(2)}, u32[]{:S(2)}) collective-permute-start(bf16[4,64,1024]{2,1,0:T(8,128)(2,1)S(1)} %all_gather.3.own_ref), channel_id=1, source_target_pairs={{0,30},{2,0},{4,2},{6,4},{8,6},{10,8},{12,10},{14,12},{16,14},{18,... | collective-permute-start | bytes 1572872 | tf_op jit(solution)/shard_map/ppermute | solution.py:133
  65.9 1.9 %collective-permute-start.1 = (bf16[4,64,1024]{2,1,0:T(8,128)(2,1)S(1)}, bf16[4,64,1024]{2,1,0:T(8,128)(2,1)S(1)}, u32[]{:S(2)}, u32[]{:S(2)}) collective-permute-start(bf16[4,64,1024]{2,1,0:T(8,128)(2,1)S(1)} %all_gather.3.own_ref), channel_id=1, source_target_pairs={{0,2},{2,4},{4,6},{6,8},{8,10},{10,12},{12,14},{14,16},{16,18},{18... | collective-permute-start | bytes 1572872 | tf_op jit(solution)/shard_map/ppermute | solution.py:133
  67.8 3.1 %collective-permute-start.4 = (bf16[2,64,1024]{2,1,0:T(8,128)(2,1)S(1)}, bf16[2,64,1024]{2,1,0:T(8,128)(2,1)S(1)}, u32[]{:S(2)}, u32[]{:S(2)}) collective-permute-start(bf16[2,64,1024]{2,1,0:T(8,128)(2,1)S(1)} %get-tuple-element.13), channel_id=1, source_target_pairs={{0,28},{2,30},{4,0},{6,2},{8,4},{10,6},{12,8},{14,10},{16,12},{18,... | collective-permute-start | bytes 786440 | tf_op jit(solution)/shard_map/ppermute | solution.py:133
  71.0 3.1 %collective-permute-start.3 = (bf16[2,64,1024]{2,1,0:T(8,128)(2,1)S(1)}, bf16[2,64,1024]{2,1,0:T(8,128)(2,1)S(1)}, u32[]{:S(2)}, u32[]{:S(2)}) collective-permute-start(bf16[2,64,1024]{2,1,0:T(8,128)(2,1)S(1)} %get-tuple-element.14), channel_id=1, source_target_pairs={{0,4},{2,6},{4,8},{6,10},{8,12},{10,14},{12,16},{14,18},{16,20},{1... | collective-permute-start | bytes 786440 | tf_op jit(solution)/shard_map/ppermute | solution.py:133
  74.0 0.1 pad_add_fusion.place_ref
  74.1 13.8 %collective-permute-done.4.high_ref = bf16[2,64,1024]{2,1,0:T(8,128)(2,1)S(1)} collective-permute-done((bf16[2,64,1024]{2,1,0:T(8,128)(2,1)S(1)}, bf16[2,64,1024]{2,1,0:T(8,128)(2,1)S(1)}, u32[]{:S(2)}, u32[]{:S(2)}) %collective-permute-start.4) | collective-permute-done | bytes 262176 | tf_op jit(solution)/shard_map/ppermute | solution.py:133
  87.9 0.0 collective-permute-done.3.low_ref
  87.9 0.0 collective-permute-done.2.after_ref
  87.9 0.0 collective-permute-done.1.before_ref
  87.9 0.0 all-to-all-done.raw_ref
  87.9 4.9 %shard_map.17 = (f32[512,1024]{1,0:T(8,128)S(1)}, bf16[1024,1024]{1,0:T(8,128)(2,1)}) custom-call(s32[2]{0:T(128)S(1)} %pad_add_fusion.place_ref, bf16[4,64,1024]{2,1,0:T(8,128)(2,1)S(1)} %all_gather.3.own_ref, bf16[4,64,1024]{2,1,0:T(8,128)(2,1)S(1)} %collective-permute-done.1.before_ref, bf16[4,64,1024]{2,1,0:T(8,128)(2,1)S(1)} %collective-permute-done.2.after_ref, ...), custom_call_target="tpu_custom_call" | custom-call | tf_op jit(solution)/shard_map/pallas_call | solution.py:89
  92.8 7.2 %collective-permute-start.6 = (f32[512,1024]{1,0:T(8,128)S(1)}, f32[512,1024]{1,0:T(8,128)S(1)}, u32[]{:S(2)}, u32[]{:S(2)}) collective-permute-start(f32[512,1024]{1,0:T(8,128)S(1)} %get-tuple-element.12), channel_id=1, source_target_pairs={{0,1},{1,0},{2,3},{3,2},{4,5},{5,4},{6,7},{7,6},{8,9},{9,8},{10,11... | collective-permute-start | bytes 6291464 | tf_op jit(solution)/shard_map/ppermute | solution.py:155
  100.0 3.8 %shard_map.18 = f32[512,1024]{1,0:T(8,128)S(1)} custom-call(s32[2]{0:T(128)S(1)} %pad_add_fusion.place_ref, bf16[4,64,1024]{2,1,0:T(8,128)(2,1)S(1)} %all_gather.3.own_ref, bf16[4,64,1024]{2,1,0:T(8,128)(2,1)S(1)} %collective-permute-done.1.before_ref, bf16[4,64,1024]{2,1,0:T(8,128)(2,1)S(1)} %collective-permute-done.2.after_ref, ...), custom_call_target="tpu_custom_call" | custom-call | tf_op jit(solution)/shard_map/pallas_call | solution.py:108
  103.8 0.0 collective-permute-done.6
  103.8 1.7 %add.3 = f32[512,1024]{1,0:T(8,128)} add(f32[512,1024]{1,0:T(8,128)S(1)} %shard_map.18, f32[512,1024]{1,0:T(8,128)S(1)} %collective-permute-done.6) | non-fusion elementwise | flops 524288 | bytes 6291456 | tf_op jit(solution)/shard_map/add | solution.py:155
  (1 shorter events, 0.0 us)
Async XLA Ops:
  0.0 32.0 %collective-permute-start = (bf16[64,1024]{1,0:T(8,128)(2,1)}, bf16[64,1024]{1,0:T(8,128)(2,1)S(1)}, u32[]{:S(2)}, u32[]{:S(2)}) collective-permute-start(bf16[64,1024]{1,0:T(8,128)(2,1)} %bitcast.3), channel_id=1, source_target_pairs={{0,0},{2,34},{4,68},{6,102},{8,136},{10,170},{12,204},{14,238},{16... | collective-permute-start | bytes 393224 | tf_op jit(solution)/shard_map/ppermute | solution.py:140
  32.0 0.7 collective-permute-start.5
  34.3 53.6 %all-to-all-start = ((bf16[16,64,1024]{2,1,0:T(8,128)(2,1)}), bf16[16,64,1024]{2,1,0:T(8,128)(2,1)}, u32[]{:S(2)}, u32[]{:S(2)}) async-start(bf16[16,64,1024]{2,1,0:T(8,128)(2,1)} %broadcast_in_dim.2), calls=%async_computation | async-start | bytes 4194304 | tf_op jit(solution)/shard_map/all_to_all | solution.py:146
  58.8 29.1 %collective-permute-start.2 = (bf16[4,64,1024]{2,1,0:T(8,128)(2,1)S(1)}, bf16[4,64,1024]{2,1,0:T(8,128)(2,1)S(1)}, u32[]{:S(2)}, u32[]{:S(2)}) collective-permute-start(bf16[4,64,1024]{2,1,0:T(8,128)(2,1)S(1)} %all_gather.3.own_ref), channel_id=1, source_target_pairs={{0,30},{2,0},{4,2},{6,4},{8,6},{10,8},{12,10},{14,12},{16,14},{18,... | collective-permute-start | bytes 1572872 | tf_op jit(solution)/shard_map/ppermute | solution.py:133
  65.9 22.0 %collective-permute-start.1 = (bf16[4,64,1024]{2,1,0:T(8,128)(2,1)S(1)}, bf16[4,64,1024]{2,1,0:T(8,128)(2,1)S(1)}, u32[]{:S(2)}, u32[]{:S(2)}) collective-permute-start(bf16[4,64,1024]{2,1,0:T(8,128)(2,1)S(1)} %all_gather.3.own_ref), channel_id=1, source_target_pairs={{0,2},{2,4},{4,6},{6,8},{8,10},{10,12},{12,14},{14,16},{16,18},{18... | collective-permute-start | bytes 1572872 | tf_op jit(solution)/shard_map/ppermute | solution.py:133
  67.8 20.0 %collective-permute-start.4 = (bf16[2,64,1024]{2,1,0:T(8,128)(2,1)S(1)}, bf16[2,64,1024]{2,1,0:T(8,128)(2,1)S(1)}, u32[]{:S(2)}, u32[]{:S(2)}) collective-permute-start(bf16[2,64,1024]{2,1,0:T(8,128)(2,1)S(1)} %get-tuple-element.13), channel_id=1, source_target_pairs={{0,28},{2,30},{4,0},{6,2},{8,4},{10,6},{12,8},{14,10},{16,12},{18,... | collective-permute-start | bytes 786440 | tf_op jit(solution)/shard_map/ppermute | solution.py:133
  71.0 16.9 %collective-permute-start.3 = (bf16[2,64,1024]{2,1,0:T(8,128)(2,1)S(1)}, bf16[2,64,1024]{2,1,0:T(8,128)(2,1)S(1)}, u32[]{:S(2)}, u32[]{:S(2)}) collective-permute-start(bf16[2,64,1024]{2,1,0:T(8,128)(2,1)S(1)} %get-tuple-element.14), channel_id=1, source_target_pairs={{0,4},{2,6},{4,8},{6,10},{8,12},{10,14},{12,16},{14,18},{16,20},{1... | collective-permute-start | bytes 786440 | tf_op jit(solution)/shard_map/ppermute | solution.py:133
  92.8 11.0 %collective-permute-start.6 = (f32[512,1024]{1,0:T(8,128)S(1)}, f32[512,1024]{1,0:T(8,128)S(1)}, u32[]{:S(2)}, u32[]{:S(2)}) collective-permute-start(f32[512,1024]{1,0:T(8,128)S(1)} %get-tuple-element.12), channel_id=1, source_target_pairs={{0,1},{1,0},{2,3},{3,2},{4,5},{5,4},{6,7},{7,6},{8,9},{9,8},{10,11... | collective-permute-start | bytes 6291464 | tf_op jit(solution)/shard_map/ppermute | solution.py:155

commit v2 on v0

v2 whole, which is shorter than its diff:
```python
import jax
import jax.numpy as jnp
from jax import lax
from jax.experimental import pallas as pl
from jax.experimental.pallas import tpu as pltpu
from jax.sharding import PartitionSpec as P

STRIDE = 4
CHUNKS = 4


def interleave(pieces):
    count, rows, width = pieces.shape
    return pieces.transpose(1, 0, 2).reshape(count * rows, width)


def order_rows(place_ref, groups, rows_ref, half):
    pieces = len(groups) * groups[0].shape[0]
    piece_rows = rows_ref.shape[0] // pieces
    start = pl.multiple_of(half * piece_rows, piece_rows)
    col = place_ref[0]
    outward = 1 - 2 * place_ref[1]
    for ref, steps in zip(groups, (0, -1, 1, -2)):
        for g, far_steps in enumerate((0, -1, 1, -2)):
            hops = steps + STRIDE * far_steps
            piece = lax.rem(col + outward * hops + pieces, pieces)
            rows_ref[pl.ds(pl.multiple_of(piece * piece_rows, piece_rows), piece_rows), :] = ref[
                g, pl.ds(start, piece_rows), :
            ]


def half_product(place_ref, rows, cols, pieces):
    tile = lax.dot_general(
        rows, cols, (((1,), (1,)), ((), ())), preferred_element_type=jnp.float32
    )
    tile = tile * (2 * place_ref[1] - 1).astype(jnp.float32)
    return interleave(tile.reshape(pieces, tile.shape[0] // pieces, tile.shape[1]))


def send_kernel(
    place_ref, own_ref, before_ref, after_ref, far_ref, raw_ref,
    out_ref, cols_ref, rows_scr, turned_scr,
):
    pieces, ex_dev, _ = raw_ref.shape
    depth = place_ref[1]
    groups = (own_ref, before_ref, after_ref, far_ref)
    order_rows(place_ref, groups, rows_scr, 1 - depth)
    first = place_ref[0] + depth * (pieces // 2)
    part = ex_dev // CHUNKS
    width = part * pieces
    for n in range(CHUNKS):
        for j in range(pieces):
            turned_scr[n, j] = raw_ref[lax.rem(first + j, pieces), n * part : (n + 1) * part, :]
        cols = interleave(turned_scr[n])
        cols_ref[n * width : (n + 1) * width, :] = cols
        out_ref[:, n * width : (n + 1) * width] = half_product(
            place_ref, rows_scr[...], cols, pieces
        )


def keep_kernel(
    place_ref, own_ref, before_ref, after_ref, far_ref, cols_ref, out_ref, rows_scr,
):
    groups = (own_ref, before_ref, after_ref, far_ref)
    order_rows(place_ref, groups, rows_scr, place_ref[1])
    pieces = STRIDE * own_ref.shape[0]
    width = cols_ref.shape[0] // CHUNKS
    for n in range(CHUNKS):
        out_ref[:, n * width : (n + 1) * width] = half_product(
            place_ref, rows_scr[...], cols_ref[n * width : (n + 1) * width, :], pieces
        )


def partial_products(place, groups, raw):
    pieces, ex_dev, feat_width = raw.shape
    width = pieces * ex_dev
    half = width // 2
    in_smem = pl.BlockSpec(memory_space=pltpu.SMEM)
    whole = pl.BlockSpec(memory_space=pltpu.VMEM)
    params = pltpu.CompilerParams(vmem_limit_bytes=24 << 20)
    product = jax.ShapeDtypeStruct((half, width), jnp.float32)
    rows_scr = pltpu.VMEM((half, feat_width), jnp.bfloat16)
    sent, cols = pl.pallas_call(
        send_kernel,
        out_shape=(product, jax.ShapeDtypeStruct((width, feat_width), jnp.bfloat16)),
        in_specs=[in_smem] + [whole] * (len(groups) + 1),
        out_specs=(whole, whole),
        scratch_shapes=[
            rows_scr,
            pltpu.VMEM((CHUNKS, pieces, ex_dev // CHUNKS, feat_width), jnp.bfloat16),
        ],
        compiler_params=params,
    )(place, *groups, raw)
    kept = pl.pallas_call(
        keep_kernel,
        out_shape=product,
        in_specs=[in_smem] + [whole] * (len(groups) + 1),
        out_specs=whole,
        scratch_shapes=[rows_scr],
        compiler_params=params,
    )(place, *groups, cols)
    return sent, kept


def body(features):
    rows_of = lax.axis_size("row")
    cols_of = lax.axis_size("col")
    own = features[0]
    ex_dev, feat_width = own.shape
    col = lax.axis_index("col").astype(jnp.int32)
    depth = lax.axis_index("depth").astype(jnp.int32)

    def at(r, c, d):
        return (r % rows_of * cols_of + c % cols_of) * 2 + d

    everywhere = [(r, c, d) for r in range(rows_of) for c in range(cols_of) for d in range(2)]
    turn = rows_of // 2
    spread = [(at(r, c, d), at(r + c + turn * d, c, d)) for r, c, d in everywhere]
    mirror = [(at(q, c, d), at(q, q - turn * d - c, d)) for q, c, d in everywhere]
    axes = ("row", "col", "depth")

    def along(value, by):
        hops = [(at(r, c, d), at(r, c + by * (1 - 2 * d), d)) for r, c, d in everywhere]
        return lax.ppermute(value, axes, hops)

    piece = lax.ppermute(own, axes, spread)
    behind = along(own, STRIDE)
    ahead = along(own, -STRIDE)
    piece, behind = lax.optimization_barrier((piece, behind))
    piece = lax.ppermute(piece, axes, mirror)
    across = along(behind, STRIDE)
    piece, behind, ahead, across = lax.optimization_barrier((piece, behind, ahead, across))
    copies = jnp.broadcast_to(piece[None], (rows_of, ex_dev, feat_width))
    raw = lax.all_to_all(copies, "row", split_axis=0, concat_axis=0, tiled=True)

    held = jnp.stack([own, behind, ahead, across])
    before = along(held, 1)
    after = along(held, -1)
    far = along(before, 1)

    place = jnp.stack([col, depth])
    sent, kept = partial_products(place, (held, before, after, far), raw)
    return kept + lax.ppermute(sent, "depth", [(0, 1), (1, 0)])


def solution(mesh):
    placed = (P("depth", ("row", "col"), None),)
    return jax.shard_map(
        body, mesh=mesh, in_specs=placed, out_specs=P(("row", "depth"), "col"), check_vma=False
    )
```

time: 266 us -> 95.4 us (0.36)
  waiting for transfers between devices: 211 us -> 26.4 us
  starting transfers between devices: 0.09 us -> 59.1 us
  blocking collectives: 27.5 us -> 0 us
  between operations: 13.1 us -> 0.14 us
  matrix products: 5.9 us -> 0 us
  Pallas kernels: 0 us -> 5.78 us
  local copies, waits for them, and re-layouts: 4.54 us -> 1.58 us
    psum x1 -> x0, waiting for transfers between devices: 126 us -> none  [broadcast(): return lax.psum(kept, axis)]
    all_gather x1 -> x0, waiting for transfers between devices: 60.2 us -> none  [body(): lax.all_gather(row_piece.reshape(ex_dev, feat_width), 'col', axis=0, tile...]
    ppermute x0 -> x9, starting transfers between devices: none -> 50.9 us  [the longest x6 29.1 us: along(): return lax.ppermute(value, axes, hops)]
    all_to_all x1 -> x0, blocking collectives: 27.5 us -> none  [body(): lax.all_to_all(grouped, 'col', split_axis=0, concat_axis=2, tiled=True)]
    reduce_scatter x1 -> x0, waiting for transfers between devices: 24.6 us -> none  [body(): lax.psum_scatter(signum * transposed_product(row_block, col_block), 'dept...]
    ppermute x0 -> x9, waiting for transfers between devices: none -> 22.7 us  [the longest x6 16.1 us: along(): return lax.ppermute(value, axes, hops)]
    all_to_all x0 -> x1, starting transfers between devices: none -> 8.2 us  [body(): raw = lax.all_to_all(copies, 'row', split_axis=0, concat_axis=0, tiled=True)]
    dot_general x1 -> x0, matrix products: 5.9 us -> none  [transposed_product(): lax.dot_general(left_rows, right_rows, (((1,), (1,)), ((), ())), preferre...]
  transfers between devices with their start and end apart: 3 -> 10, of which waited for: 3 -> 8; matrix products, arithmetic and copies ran while one was open for 0% -> 0% of each run, Pallas kernels for 0% -> 3%
where the time goes in v2:
time: 95.4 us; the launch traced here: 94.9 us
  starting transfers between devices  59.1 us (62%)
  waiting for transfers between devices  26.4 us (28%)
  Pallas kernels  5.78 us (6%)
  other arithmetic  2.02 us (2%)
  local copies, waits for them, and re-layouts  1.58 us (2%)
    ppermute x6, starting transfers between devices, along(): return lax.ppermute(value, axes, hops)  29.1 us
    ppermute x6, waiting for transfers between devices, along(): return lax.ppermute(value, axes, hops)  16.1 us
    ppermute x1, starting transfers between devices, body(): piece = lax.ppermute(piece, axes, mirror)  9.88 us
    all_to_all x1, starting transfers between devices, body(): raw = lax.all_to_all(copies, 'row', split_axis=0, concat_axis=0, tiled=True)  8.2 us
    ppermute x1, starting transfers between devices, body(): return kept + lax.ppermute(sent, 'depth', [(0, 1), (1, 0)])  7.07 us
    ppermute x1, waiting for transfers between devices, body(): piece = lax.ppermute(piece, axes, mirror)  4.98 us
    ppermute x1, starting transfers between devices, body(): piece = lax.ppermute(own, axes, spread)  4.82 us
    all_to_all x1, waiting for transfers between devices, body(): raw = lax.all_to_all(copies, 'row', split_axis=0, concat_axis=0, tiled=True)  3.65 us
  transfers between devices with their start and end apart: 10, of which 8 were waited for; matrix products, arithmetic and copies ran while one was open for 0% of the time, Pallas kernels for 3%

profile of v2, /device:TPU:1, one launch (start us, length us, event | category | flops | bytes accessed | tf_op | source)
XLA Modules:
  0.0 94.9 jit_solution(17184266915706558888)
XLA Ops:
  0.0 13.3 %collective-permute-start.1 = (bf16[64,1024]{1,0:T(8,128)(2,1)}, bf16[64,1024]{1,0:T(8,128)(2,1)S(1)}, u32[]{:S(2)}, u32[]{:S(2)}) collective-permute-start(bf16[64,1024]{1,0:T(8,128)(2,1)} %bitcast.6), channel_id=1, source_target_pairs={{0,8},{1,25},{2,10},{3,27},{4,12},{5,29},{6,14},{7,31},{8,16},{9,1... | collective-permute-start | bytes 393224 | tf_op jit(solution)/shard_map/ppermute | solution.py:124
  13.3 4.8 %collective-permute-start = (bf16[64,1024]{1,0:T(8,128)(2,1)}, bf16[64,1024]{1,0:T(8,128)(2,1)S(1)}, u32[]{:S(2)}, u32[]{:S(2)}) collective-permute-start(bf16[64,1024]{1,0:T(8,128)(2,1)} %bitcast.7), channel_id=1, source_target_pairs={{0,0},{1,257},{2,34},{3,291},{4,68},{5,325},{6,102},{7,359},{8,136... | collective-permute-start | bytes 393224 | tf_op jit(solution)/shard_map/ppermute | solution.py:126
  18.1 1.9 %collective-permute-start.3 = (bf16[64,1024]{1,0:T(8,128)(2,1)}, bf16[64,1024]{1,0:T(8,128)(2,1)S(1)}, u32[]{:S(2)}, u32[]{:S(2)}) collective-permute-start(bf16[64,1024]{1,0:T(8,128)(2,1)} %bitcast.8), channel_id=1, source_target_pairs={{0,24},{1,9},{2,26},{3,11},{4,28},{5,13},{6,30},{7,15},{8,0},{9,17... | collective-permute-start | bytes 393224 | tf_op jit(solution)/shard_map/ppermute | solution.py:124
  20.1 0.7 collective-permute-done
  20.7 9.9 %collective-permute-start.2 = (bf16[64,1024]{1,0:T(8,128)(2,1)S(1)}, bf16[64,1024]{1,0:T(8,128)(2,1)S(1)}, u32[]{:S(2)}, u32[]{:S(2)}) collective-permute-start(bf16[64,1024]{1,0:T(8,128)(2,1)S(1)} %collective-permute-done), channel_id=1, source_target_pairs={{0,0},{1,17},{2,30},{3,15},{4,28},{5,13},{6,26},{7,11},{8,24},{9,9... | collective-permute-start | bytes 393224 | tf_op jit(solution)/shard_map/ppermute | solution.py:130
  30.6 1.9 %collective-permute-start.4 = (bf16[64,1024]{1,0:T(8,128)(2,1)S(1)}, bf16[64,1024]{1,0:T(8,128)(2,1)S(1)}, u32[]{:S(2)}, u32[]{:S(2)}) collective-permute-start(bf16[64,1024]{1,0:T(8,128)(2,1)S(1)} %collective-permute-done.1), channel_id=1, source_target_pairs={{0,8},{1,25},{2,10},{3,27},{4,12},{5,29},{6,14},{7,31},{8,16},{9,1... | collective-permute-start | bytes 393224 | tf_op jit(solution)/shard_map/ppermute | solution.py:124
  32.5 5.0 %collective-permute-done.2 = bf16[64,1024]{1,0:T(8,128)(2,1)S(1)} collective-permute-done((bf16[64,1024]{1,0:T(8,128)(2,1)S(1)}, bf16[64,1024]{1,0:T(8,128)(2,1)S(1)}, u32[]{:S(2)}, u32[]{:S(2)}) %collective-permute-start.2) | collective-permute-done | bytes 131104 | tf_op jit(solution)/shard_map/ppermute | solution.py:130
  37.5 4.3 %collective-permute-done.4 = bf16[64,1024]{1,0:T(8,128)(2,1)S(1)} collective-permute-done((bf16[64,1024]{1,0:T(8,128)(2,1)S(1)}, bf16[64,1024]{1,0:T(8,128)(2,1)S(1)}, u32[]{:S(2)}, u32[]{:S(2)}) %collective-permute-start.4) | collective-permute-done | bytes 131104 | tf_op jit(solution)/shard_map/ppermute | solution.py:124
  41.8 1.6 %broadcast_in_dim.2 = bf16[16,64,1024]{2,1,0:T(8,128)(2,1)} broadcast(bf16[64,1024]{1,0:T(8,128)(2,1)S(1)} %collective-permute-done.2), dimensions={1,2} | broadcast | bytes 2228224 | tf_op jit(solution)/shard_map/broadcast_in_dim | solution.py:133
  43.4 8.2 %all-to-all-start = ((bf16[16,64,1024]{2,1,0:T(8,128)(2,1)}), bf16[16,64,1024]{2,1,0:T(8,128)(2,1)S(1)}, u32[]{:S(2)}, u32[]{:S(2)}) async-start(bf16[16,64,1024]{2,1,0:T(8,128)(2,1)} %broadcast_in_dim.2), calls=%async_computation | async-start | bytes 4194304 | tf_op jit(solution)/shard_map/all_to_all | solution.py:134
  51.6 0.1 pad_maximum_fusion.own_ref
  51.7 4.7 %collective-permute-start.5 = (bf16[4,64,1024]{2,1,0:T(8,128)(2,1)S(1)}, bf16[4,64,1024]{2,1,0:T(8,128)(2,1)S(1)}, u32[]{:S(2)}, u32[]{:S(2)}) collective-permute-start(bf16[4,64,1024]{2,1,0:T(8,128)(2,1)S(1)} %pad_maximum_fusion.own_ref), channel_id=1, source_target_pairs={{0,2},{1,31},{2,4},{3,1},{4,6},{5,3},{6,8},{7,5},{8,10},{9,7},{10,... | collective-permute-start | bytes 1572872 | tf_op jit(solution)/shard_map/ppermute | solution.py:124
  56.5 1.9 %collective-permute-start.6 = (bf16[4,64,1024]{2,1,0:T(8,128)(2,1)S(1)}, bf16[4,64,1024]{2,1,0:T(8,128)(2,1)}, u32[]{:S(2)}, u32[]{:S(2)}) collective-permute-start(bf16[4,64,1024]{2,1,0:T(8,128)(2,1)S(1)} %pad_maximum_fusion.own_ref), channel_id=1, source_target_pairs={{0,30},{1,3},{2,0},{3,5},{4,2},{5,7},{6,4},{7,9},{8,6},{9,11},{10,... | collective-permute-start | bytes 1572872 | tf_op jit(solution)/shard_map/ppermute | solution.py:124
  58.4 4.2 %collective-permute-done.5.before_ref = bf16[4,64,1024]{2,1,0:T(8,128)(2,1)S(1)} collective-permute-done((bf16[4,64,1024]{2,1,0:T(8,128)(2,1)S(1)}, bf16[4,64,1024]{2,1,0:T(8,128)(2,1)S(1)}, u32[]{:S(2)}, u32[]{:S(2)}) %collective-permute-start.5) | collective-permute-done | bytes 524320 | tf_op jit(solution)/shard_map/ppermute | solution.py:124
  62.6 5.3 %collective-permute-start.7 = (bf16[4,64,1024]{2,1,0:T(8,128)(2,1)S(1)}, bf16[4,64,1024]{2,1,0:T(8,128)(2,1)}, u32[]{:S(2)}, u32[]{:S(2)}) collective-permute-start(bf16[4,64,1024]{2,1,0:T(8,128)(2,1)S(1)} %collective-permute-done.5.before_ref), channel_id=1, source_target_pairs={{0,2},{1,31},{2,4},{3,1},{4,6},{5,3},{6,8},{7,5},{8,10},{9,7},{10,... | collective-permute-start | bytes 1572872 | tf_op jit(solution)/shard_map/ppermute | solution.py:124
  67.9 0.1 pad_add_fusion.place_ref
  68.0 4.6 %collective-permute-done.6.after_ref = bf16[4,64,1024]{2,1,0:T(8,128)(2,1)} collective-permute-done((bf16[4,64,1024]{2,1,0:T(8,128)(2,1)S(1)}, bf16[4,64,1024]{2,1,0:T(8,128)(2,1)}, u32[]{:S(2)}, u32[]{:S(2)}) %collective-permute-start.6) | collective-permute-done | bytes 524320 | tf_op jit(solution)/shard_map/ppermute | solution.py:124
  72.6 3.0 %collective-permute-done.7.far_ref = bf16[4,64,1024]{2,1,0:T(8,128)(2,1)} collective-permute-done((bf16[4,64,1024]{2,1,0:T(8,128)(2,1)S(1)}, bf16[4,64,1024]{2,1,0:T(8,128)(2,1)}, u32[]{:S(2)}, u32[]{:S(2)}) %collective-permute-start.7) | collective-permute-done | bytes 524320 | tf_op jit(solution)/shard_map/ppermute | solution.py:124
  75.6 3.6 %all-to-all-done.raw_ref = bf16[16,64,1024]{2,1,0:T(8,128)(2,1)S(1)} async-done(((bf16[16,64,1024]{2,1,0:T(8,128)(2,1)}), bf16[16,64,1024]{2,1,0:T(8,128)(2,1)S(1)}, u32[]{:S(2)}, u32[]{:S(2)}) %all-to-all-start) | async-done | bytes 2097184 | tf_op jit(solution)/shard_map/all_to_all | solution.py:134
  79.3 3.0 %shard_map.17 = (f32[512,1024]{1,0:T(8,128)S(1)}, bf16[1024,1024]{1,0:T(8,128)(2,1)S(1)}) custom-call(s32[2]{0:T(128)S(1)} %pad_add_fusion.place_ref, bf16[4,64,1024]{2,1,0:T(8,128)(2,1)S(1)} %pad_maximum_fusion.own_ref, bf16[4,64,1024]{2,1,0:T(8,128)(2,1)S(1)} %collective-permute-done.5.before_ref, bf16[4,64,1024]{2,1,0:T(8,128)(2,1)} %collective-permute-done.6.after_ref, ...), custom_call_target="tpu_custom_call" | custom-call | tf_op jit(solution)/shard_map/pallas_call | solution.py:83
  82.2 7.1 %collective-permute-start.8 = (f32[512,1024]{1,0:T(8,128)S(1)}, f32[512,1024]{1,0:T(8,128)S(1)}, u32[]{:S(2)}, u32[]{:S(2)}) collective-permute-start(f32[512,1024]{1,0:T(8,128)S(1)} %get-tuple-element.20), channel_id=1, source_target_pairs={{0,1},{1,0},{2,3},{3,2},{4,5},{5,4},{6,7},{7,6},{8,9},{9,8},{10,11... | collective-permute-start | bytes 6291464 | tf_op jit(solution)/shard_map/ppermute | solution.py:143
  89.3 2.8 %shard_map.18 = f32[512,1024]{1,0:T(8,128)S(1)} custom-call(s32[2]{0:T(128)S(1)} %pad_add_fusion.place_ref, bf16[4,64,1024]{2,1,0:T(8,128)(2,1)S(1)} %pad_maximum_fusion.own_ref, bf16[4,64,1024]{2,1,0:T(8,128)(2,1)S(1)} %collective-permute-done.5.before_ref, bf16[4,64,1024]{2,1,0:T(8,128)(2,1)} %collective-permute-done.6.after_ref, ...), custom_call_target="tpu_custom_call" | custom-call | tf_op jit(solution)/shard_map/pallas_call | solution.py:94
  92.1 0.9 collective-permute-done.8
  93.1 1.9 %add.3 = f32[512,1024]{1,0:T(8,128)} add(f32[512,1024]{1,0:T(8,128)S(1)} %shard_map.18, f32[512,1024]{1,0:T(8,128)S(1)} %collective-permute-done.8) | non-fusion elementwise | flops 524288 | bytes 6291456 | tf_op jit(solution)/shard_map/add | solution.py:143
  (4 shorter events, 0.0 us)
Async XLA Ops:
  0.0 20.0 %collective-permute-start.1 = (bf16[64,1024]{1,0:T(8,128)(2,1)}, bf16[64,1024]{1,0:T(8,128)(2,1)S(1)}, u32[]{:S(2)}, u32[]{:S(2)}) collective-permute-start(bf16[64,1024]{1,0:T(8,128)(2,1)} %bitcast.6), channel_id=1, source_target_pairs={{0,8},{1,25},{2,10},{3,27},{4,12},{5,29},{6,14},{7,31},{8,16},{9,1... | collective-permute-start | bytes 393224 | tf_op jit(solution)/shard_map/ppermute | solution.py:124
  13.3 7.4 %collective-permute-start = (bf16[64,1024]{1,0:T(8,128)(2,1)}, bf16[64,1024]{1,0:T(8,128)(2,1)S(1)}, u32[]{:S(2)}, u32[]{:S(2)}) collective-permute-start(bf16[64,1024]{1,0:T(8,128)(2,1)} %bitcast.7), channel_id=1, source_target_pairs={{0,0},{1,257},{2,34},{3,291},{4,68},{5,325},{6,102},{7,359},{8,136... | collective-permute-start | bytes 393224 | tf_op jit(solution)/shard_map/ppermute | solution.py:126
  18.1 14.4 %collective-permute-start.3 = (bf16[64,1024]{1,0:T(8,128)(2,1)}, bf16[64,1024]{1,0:T(8,128)(2,1)S(1)}, u32[]{:S(2)}, u32[]{:S(2)}) collective-permute-start(bf16[64,1024]{1,0:T(8,128)(2,1)} %bitcast.8), channel_id=1, source_target_pairs={{0,24},{1,9},{2,26},{3,11},{4,28},{5,13},{6,30},{7,15},{8,0},{9,17... | collective-permute-start | bytes 393224 | tf_op jit(solution)/shard_map/ppermute | solution.py:124
  20.7 16.8 %collective-permute-start.2 = (bf16[64,1024]{1,0:T(8,128)(2,1)S(1)}, bf16[64,1024]{1,0:T(8,128)(2,1)S(1)}, u32[]{:S(2)}, u32[]{:S(2)}) collective-permute-start(bf16[64,1024]{1,0:T(8,128)(2,1)S(1)} %collective-permute-done), channel_id=1, source_target_pairs={{0,0},{1,17},{2,30},{3,15},{4,28},{5,13},{6,26},{7,11},{8,24},{9,9... | collective-permute-start | bytes 393224 | tf_op jit(solution)/shard_map/ppermute | solution.py:130
  30.6 11.2 %collective-permute-start.4 = (bf16[64,1024]{1,0:T(8,128)(2,1)S(1)}, bf16[64,1024]{1,0:T(8,128)(2,1)S(1)}, u32[]{:S(2)}, u32[]{:S(2)}) collective-permute-start(bf16[64,1024]{1,0:T(8,128)(2,1)S(1)} %collective-permute-done.1), channel_id=1, source_target_pairs={{0,8},{1,25},{2,10},{3,27},{4,12},{5,29},{6,14},{7,31},{8,16},{9,1... | collective-permute-start | bytes 393224 | tf_op jit(solution)/shard_map/ppermute | solution.py:124
  43.4 8.2 %copy-start = (bf16[1,64,1024]{2,1,0:T(8,128)(2,1)S(1)}, bf16[1,64,1024]{2,1,0:T(8,128)(2,1)}, u32[]{:S(2)}) copy-start(bf16[1,64,1024]{2,1,0:T(8,128)(2,1)} %param.1) | copy-start | bytes 393220
  43.4 35.8 %all-to-all-start = ((bf16[16,64,1024]{2,1,0:T(8,128)(2,1)}), bf16[16,64,1024]{2,1,0:T(8,128)(2,1)S(1)}, u32[]{:S(2)}, u32[]{:S(2)}) async-start(bf16[16,64,1024]{2,1,0:T(8,128)(2,1)} %broadcast_in_dim.2), calls=%async_computation | async-start | bytes 4194304 | tf_op jit(solution)/shard_map/all_to_all | solution.py:134
  51.7 10.9 %collective-permute-start.5 = (bf16[4,64,1024]{2,1,0:T(8,128)(2,1)S(1)}, bf16[4,64,1024]{2,1,0:T(8,128)(2,1)S(1)}, u32[]{:S(2)}, u32[]{:S(2)}) collective-permute-start(bf16[4,64,1024]{2,1,0:T(8,128)(2,1)S(1)} %pad_maximum_fusion.own_ref), channel_id=1, source_target_pairs={{0,2},{1,31},{2,4},{3,1},{4,6},{5,3},{6,8},{7,5},{8,10},{9,7},{10,... | collective-permute-start | bytes 1572872 | tf_op jit(solution)/shard_map/ppermute | solution.py:124
  56.5 16.1 %collective-permute-start.6 = (bf16[4,64,1024]{2,1,0:T(8,128)(2,1)S(1)}, bf16[4,64,1024]{2,1,0:T(8,128)(2,1)}, u32[]{:S(2)}, u32[]{:S(2)}) collective-permute-start(bf16[4,64,1024]{2,1,0:T(8,128)(2,1)S(1)} %pad_maximum_fusion.own_ref), channel_id=1, source_target_pairs={{0,30},{1,3},{2,0},{3,5},{4,2},{5,7},{6,4},{7,9},{8,6},{9,11},{10,... | collective-permute-start | bytes 1572872 | tf_op jit(solution)/shard_map/ppermute | solution.py:124
  62.6 13.0 %collective-permute-start.7 = (bf16[4,64,1024]{2,1,0:T(8,128)(2,1)S(1)}, bf16[4,64,1024]{2,1,0:T(8,128)(2,1)}, u32[]{:S(2)}, u32[]{:S(2)}) collective-permute-start(bf16[4,64,1024]{2,1,0:T(8,128)(2,1)S(1)} %collective-permute-done.5.before_ref), channel_id=1, source_target_pairs={{0,2},{1,31},{2,4},{3,1},{4,6},{5,3},{6,8},{7,5},{8,10},{9,7},{10,... | collective-permute-start | bytes 1572872 | tf_op jit(solution)/shard_map/ppermute | solution.py:124
  82.2 10.8 %collective-permute-start.8 = (f32[512,1024]{1,0:T(8,128)S(1)}, f32[512,1024]{1,0:T(8,128)S(1)}, u32[]{:S(2)}, u32[]{:S(2)}) collective-permute-start(f32[512,1024]{1,0:T(8,128)S(1)} %get-tuple-element.20), channel_id=1, source_target_pairs={{0,1},{1,0},{2,3},{3,2},{4,5},{5,4},{6,7},{7,6},{8,9},{9,8},{10,11... | collective-permute-start | bytes 6291464 | tf_op jit(solution)/shard_map/ppermute | solution.py:143

commit v3 on v2

--- a/solution.py
+++ b/solution.py
@@ -7,6 +7,7 @@
 
 STRIDE = 4
 CHUNKS = 4
+TURN = 5
 
 
 def interleave(pieces):
@@ -50,7 +51,7 @@
     width = part * pieces
     for n in range(CHUNKS):
         for j in range(pieces):
-            turned_scr[n, j] = raw_ref[lax.rem(first + j, pieces), n * part : (n + 1) * part, :]
+            turned_scr[n, j] = raw_ref[lax.rem(first + (pieces - TURN) * j, pieces), n * part : (n + 1) * part, :]
         cols = interleave(turned_scr[n])
         cols_ref[n * width : (n + 1) * width, :] = cols
         out_ref[:, n * width : (n + 1) * width] = half_product(
@@ -69,6 +70,36 @@
         out_ref[:, n * width : (n + 1) * width] = half_product(
             place_ref, rows_scr[...], cols_ref[n * width : (n + 1) * width, :], pieces
         )
+
+
+def finish_kernel(kept_ref, came_ref, out_ref, sum_scr, sems):
+    parts, rows, _ = sum_scr.shape
+    stores = []
+    for n in range(parts):
+        band = pl.ds(n * rows, rows)
+        sum_scr[n] = kept_ref[band, :] + came_ref[band, :]
+        store = pltpu.make_async_copy(sum_scr.at[n], out_ref.at[band, :], sems.at[n])
+        store.start()
+        stores.append(store)
+    for store in stores:
+        store.wait()
+
+
+def finished(kept, came):
+    rows, width = kept.shape
+    parts = 8
+    whole = pl.BlockSpec(memory_space=pltpu.VMEM)
+    return pl.pallas_call(
+        finish_kernel,
+        out_shape=jax.ShapeDtypeStruct((rows, width), jnp.float32),
+        in_specs=[whole, whole],
+        out_specs=pl.BlockSpec(memory_space=pltpu.HBM),
+        scratch_shapes=[
+            pltpu.VMEM((parts, rows // parts, width), jnp.float32),
+            pltpu.SemaphoreType.DMA((parts,)),
+        ],
+        compiler_params=pltpu.CompilerParams(vmem_limit_bytes=16 << 20),
+    )(kept, came)
 
 
 def partial_products(place, groups, raw):
@@ -115,8 +146,8 @@
 
     everywhere = [(r, c, d) for r in range(rows_of) for c in range(cols_of) for d in range(2)]
     turn = rows_of // 2
-    spread = [(at(r, c, d), at(r + c + turn * d, c, d)) for r, c, d in everywhere]
-    mirror = [(at(q, c, d), at(q, q - turn * d - c, d)) for q, c, d in everywhere]
+    spread = [(at(r, c, d), at(r - TURN * c + turn * d, c, d)) for r, c, d in everywhere]
+    mirror = [(at(q, c, d), at(q, q - turn * d + TURN * c, d)) for q, c, d in everywhere]
     axes = ("row", "col", "depth")
 
     def along(value, by):
@@ -140,7 +171,7 @@
 
     place = jnp.stack([col, depth])
     sent, kept = partial_products(place, (held, before, after, far), raw)
-    return kept + lax.ppermute(sent, "depth", [(0, 1), (1, 0)])
+    return finished(kept, lax.ppermute(sent, "depth", [(0, 1), (1, 0)]))
 
 
 def solution(mesh):

time: 95.4 us -> 94.7 us (level)
  other arithmetic: 2.02 us -> 0.15 us
  Pallas kernels: 5.78 us -> 7.18 us
  starting transfers between devices: 59.1 us -> 57.9 us
    ppermute x6, starting transfers between devices: 29.1 us -> 25.5 us  [along(): return lax.ppermute(value, axes, hops)]
    ppermute x6, waiting for transfers between devices: 16.1 us -> 18.9 us  [along(): return lax.ppermute(value, axes, hops)]
    all_to_all x1, waiting for transfers between devices: 3.65 us -> 1.17 us  [body(): raw = lax.all_to_all(copies, 'row', split_axis=0, concat_axis=0, tiled=True)]
    ppermute x1, starting transfers between devices: 7.07 us -> 8.97 us  [body(): return finished(kept, lax.ppermute(sent, 'depth', [(0, 1), (1, 0)]))]
    add x1 -> x0, other arithmetic: 1.88 us -> none  [body(): return kept + lax.ppermute(sent, 'depth', [(0, 1), (1, 0)])]
    pallas_call x0 -> x1, Pallas kernels: none -> 1.4 us  [finished(): pl.pallas_call(finish_kernel, out_shape=jax.ShapeDtypeStruct((rows, width...]
where the time goes in v3:
time: 94.7 us; the launch traced here: 94.2 us
  starting transfers between devices  57.9 us (61%)
  waiting for transfers between devices  27.3 us (29%)
  Pallas kernels  7.18 us (8%)
  local copies, waits for them, and re-layouts  1.58 us (2%)
    ppermute x6, starting transfers between devices, along(): return lax.ppermute(value, axes, hops)  25.5 us
    ppermute x6, waiting for transfers between devices, along(): return lax.ppermute(value, axes, hops)  18.9 us
    ppermute x1, starting transfers between devices, body(): piece = lax.ppermute(piece, axes, mirror)  9.88 us
    ppermute x1, starting transfers between devices, body(): return finished(kept, lax.ppermute(sent, 'depth', [(0, 1), (1, 0)]))  8.97 us
    all_to_all x1, starting transfers between devices, body(): raw = lax.all_to_all(copies, 'row', split_axis=0, concat_axis=0, tiled=True)  8.73 us
    ppermute x1, waiting for transfers between devices, body(): piece = lax.ppermute(piece, axes, mirror)  5.58 us
    ppermute x1, starting transfers between devices, body(): piece = lax.ppermute(own, axes, spread)  4.82 us
    pallas_call x1, Pallas kernels, partial_products(): pl.pallas_call(send_kernel, out_shape=(product, jax.ShapeDtypeStruct((wid...  2.96 us
  transfers between devices with their start and end apart: 10, of which 8 were waited for; matrix products, arithmetic and copies ran while one was open for 0% of the time, Pallas kernels for 3%

profile of v3, /device:TPU:1, one launch (start us, length us, event | category | flops | bytes accessed | tf_op | source)
XLA Modules:
  0.0 94.2 jit_solution(14094879004841309373)
XLA Ops:
  0.0 13.3 %collective-permute-start.1 = (bf16[64,1024]{1,0:T(8,128)(2,1)}, bf16[64,1024]{1,0:T(8,128)(2,1)S(1)}, u32[]{:S(2)}, u32[]{:S(2)}) collective-permute-start(bf16[64,1024]{1,0:T(8,128)(2,1)} %bitcast.6), channel_id=1, source_target_pairs={{0,8},{1,25},{2,10},{3,27},{4,12},{5,29},{6,14},{7,31},{8,16},{9,1... | collective-permute-start | bytes 393224 | tf_op jit(solution)/shard_map/ppermute | solution.py:155
  13.3 4.8 %collective-permute-start = (bf16[64,1024]{1,0:T(8,128)(2,1)}, bf16[64,1024]{1,0:T(8,128)(2,1)S(1)}, u32[]{:S(2)}, u32[]{:S(2)}) collective-permute-start(bf16[64,1024]{1,0:T(8,128)(2,1)} %bitcast.7), channel_id=1, source_target_pairs={{0,0},{1,257},{2,354},{3,99},{4,196},{5,453},{6,38},{7,295},{8,392... | collective-permute-start | bytes 393224 | tf_op jit(solution)/shard_map/ppermute | solution.py:157
  18.1 1.9 %collective-permute-start.3 = (bf16[64,1024]{1,0:T(8,128)(2,1)}, bf16[64,1024]{1,0:T(8,128)(2,1)S(1)}, u32[]{:S(2)}, u32[]{:S(2)}) collective-permute-start(bf16[64,1024]{1,0:T(8,128)(2,1)} %bitcast.8), channel_id=1, source_target_pairs={{0,24},{1,9},{2,26},{3,11},{4,28},{5,13},{6,30},{7,15},{8,0},{9,17... | collective-permute-start | bytes 393224 | tf_op jit(solution)/shard_map/ppermute | solution.py:155
  20.1 0.7 collective-permute-done
  20.7 9.9 %collective-permute-start.2 = (bf16[64,1024]{1,0:T(8,128)(2,1)S(1)}, bf16[64,1024]{1,0:T(8,128)(2,1)S(1)}, u32[]{:S(2)}, u32[]{:S(2)}) collective-permute-start(bf16[64,1024]{1,0:T(8,128)(2,1)S(1)} %collective-permute-done), channel_id=1, source_target_pairs={{0,0},{1,17},{2,10},{3,27},{4,20},{5,5},{6,30},{7,15},{8,8},{9,25}... | collective-permute-start | bytes 393224 | tf_op jit(solution)/shard_map/ppermute | solution.py:161
  30.6 1.9 %collective-permute-start.4 = (bf16[64,1024]{1,0:T(8,128)(2,1)S(1)}, bf16[64,1024]{1,0:T(8,128)(2,1)S(1)}, u32[]{:S(2)}, u32[]{:S(2)}) collective-permute-start(bf16[64,1024]{1,0:T(8,128)(2,1)S(1)} %collective-permute-done.1), channel_id=1, source_target_pairs={{0,8},{1,25},{2,10},{3,27},{4,12},{5,29},{6,14},{7,31},{8,16},{9,1... | collective-permute-start | bytes 393224 | tf_op jit(solution)/shard_map/ppermute | solution.py:155
  32.5 5.6 %collective-permute-done.2 = bf16[64,1024]{1,0:T(8,128)(2,1)S(1)} collective-permute-done((bf16[64,1024]{1,0:T(8,128)(2,1)S(1)}, bf16[64,1024]{1,0:T(8,128)(2,1)S(1)}, u32[]{:S(2)}, u32[]{:S(2)}) %collective-permute-start.2) | collective-permute-done | bytes 131104 | tf_op jit(solution)/shard_map/ppermute | solution.py:161
  38.1 3.9 %collective-permute-done.4 = bf16[64,1024]{1,0:T(8,128)(2,1)S(1)} collective-permute-done((bf16[64,1024]{1,0:T(8,128)(2,1)S(1)}, bf16[64,1024]{1,0:T(8,128)(2,1)S(1)}, u32[]{:S(2)}, u32[]{:S(2)}) %collective-permute-start.4) | collective-permute-done | bytes 131104 | tf_op jit(solution)/shard_map/ppermute | solution.py:155
  42.0 1.6 %broadcast_in_dim.2 = bf16[16,64,1024]{2,1,0:T(8,128)(2,1)} broadcast(bf16[64,1024]{1,0:T(8,128)(2,1)S(1)} %collective-permute-done.2), dimensions={1,2} | broadcast | bytes 2228224 | tf_op jit(solution)/shard_map/broadcast_in_dim | solution.py:164
  43.6 8.7 %all-to-all-start = ((bf16[16,64,1024]{2,1,0:T(8,128)(2,1)}), bf16[16,64,1024]{2,1,0:T(8,128)(2,1)S(1)}, u32[]{:S(2)}, u32[]{:S(2)}) async-start(bf16[16,64,1024]{2,1,0:T(8,128)(2,1)} %broadcast_in_dim.2), calls=%async_computation | async-start | bytes 4194304 | tf_op jit(solution)/shard_map/all_to_all | solution.py:165
  52.4 0.1 pad_maximum_fusion.own_ref
  52.4 1.9 %collective-permute-start.5 = (bf16[4,64,1024]{2,1,0:T(8,128)(2,1)S(1)}, bf16[4,64,1024]{2,1,0:T(8,128)(2,1)S(1)}, u32[]{:S(2)}, u32[]{:S(2)}) collective-permute-start(bf16[4,64,1024]{2,1,0:T(8,128)(2,1)S(1)} %pad_maximum_fusion.own_ref), channel_id=1, source_target_pairs={{0,2},{1,31},{2,4},{3,1},{4,6},{5,3},{6,8},{7,5},{8,10},{9,7},{10,... | collective-permute-start | bytes 1572872 | tf_op jit(solution)/shard_map/ppermute | solution.py:155
  54.4 3.4 %collective-permute-start.6 = (bf16[4,64,1024]{2,1,0:T(8,128)(2,1)S(1)}, bf16[4,64,1024]{2,1,0:T(8,128)(2,1)}, u32[]{:S(2)}, u32[]{:S(2)}) collective-permute-start(bf16[4,64,1024]{2,1,0:T(8,128)(2,1)S(1)} %pad_maximum_fusion.own_ref), channel_id=1, source_target_pairs={{0,30},{1,3},{2,0},{3,5},{4,2},{5,7},{6,4},{7,9},{8,6},{9,11},{10,... | collective-permute-start | bytes 1572872 | tf_op jit(solution)/shard_map/ppermute | solution.py:155
  57.7 4.9 %collective-permute-done.5.before_ref = bf16[4,64,1024]{2,1,0:T(8,128)(2,1)S(1)} collective-permute-done((bf16[4,64,1024]{2,1,0:T(8,128)(2,1)S(1)}, bf16[4,64,1024]{2,1,0:T(8,128)(2,1)S(1)}, u32[]{:S(2)}, u32[]{:S(2)}) %collective-permute-start.5) | collective-permute-done | bytes 524320 | tf_op jit(solution)/shard_map/ppermute | solution.py:155
  62.7 3.1 %collective-permute-start.7 = (bf16[4,64,1024]{2,1,0:T(8,128)(2,1)S(1)}, bf16[4,64,1024]{2,1,0:T(8,128)(2,1)}, u32[]{:S(2)}, u32[]{:S(2)}) collective-permute-start(bf16[4,64,1024]{2,1,0:T(8,128)(2,1)S(1)} %collective-permute-done.5.before_ref), channel_id=1, source_target_pairs={{0,2},{1,31},{2,4},{3,1},{4,6},{5,3},{6,8},{7,5},{8,10},{9,7},{10,... | collective-permute-start | bytes 1572872 | tf_op jit(solution)/shard_map/ppermute | solution.py:155
  65.8 0.1 pad_add_fusion.place_ref
  65.9 2.6 %collective-permute-done.6.after_ref = bf16[4,64,1024]{2,1,0:T(8,128)(2,1)} collective-permute-done((bf16[4,64,1024]{2,1,0:T(8,128)(2,1)S(1)}, bf16[4,64,1024]{2,1,0:T(8,128)(2,1)}, u32[]{:S(2)}, u32[]{:S(2)}) %collective-permute-start.6) | collective-permute-done | bytes 524320 | tf_op jit(solution)/shard_map/ppermute | solution.py:155
  68.4 7.5 %collective-permute-done.7.far_ref = bf16[4,64,1024]{2,1,0:T(8,128)(2,1)} collective-permute-done((bf16[4,64,1024]{2,1,0:T(8,128)(2,1)S(1)}, bf16[4,64,1024]{2,1,0:T(8,128)(2,1)}, u32[]{:S(2)}, u32[]{:S(2)}) %collective-permute-start.7) | collective-permute-done | bytes 524320 | tf_op jit(solution)/shard_map/ppermute | solution.py:155
  76.0 1.2 %all-to-all-done.raw_ref = bf16[16,64,1024]{2,1,0:T(8,128)(2,1)S(1)} async-done(((bf16[16,64,1024]{2,1,0:T(8,128)(2,1)}), bf16[16,64,1024]{2,1,0:T(8,128)(2,1)S(1)}, u32[]{:S(2)}, u32[]{:S(2)}) %all-to-all-start) | async-done | bytes 2097184 | tf_op jit(solution)/shard_map/all_to_all | solution.py:165
  77.1 3.0 %shard_map.17 = (f32[512,1024]{1,0:T(8,128)S(1)}, bf16[1024,1024]{1,0:T(8,128)(2,1)S(1)}) custom-call(s32[2]{0:T(128)S(1)} %pad_add_fusion.place_ref, bf16[4,64,1024]{2,1,0:T(8,128)(2,1)S(1)} %pad_maximum_fusion.own_ref, bf16[4,64,1024]{2,1,0:T(8,128)(2,1)S(1)} %collective-permute-done.5.before_ref, bf16[4,64,1024]{2,1,0:T(8,128)(2,1)} %collective-permute-done.6.after_ref, ...), custom_call_target="tpu_custom_call" | custom-call | tf_op jit(solution)/shard_map/pallas_call | solution.py:114
  80.1 9.0 %collective-permute-start.8 = (f32[512,1024]{1,0:T(8,128)S(1)}, f32[512,1024]{1,0:T(8,128)S(1)}, u32[]{:S(2)}, u32[]{:S(2)}) collective-permute-start(f32[512,1024]{1,0:T(8,128)S(1)} %get-tuple-element.20), channel_id=1, source_target_pairs={{0,1},{1,0},{2,3},{3,2},{4,5},{5,4},{6,7},{7,6},{8,9},{9,8},{10,11... | collective-permute-start | bytes 6291464 | tf_op jit(solution)/shard_map/ppermute | solution.py:174
  89.1 2.8 %shard_map.18.kept_ref = f32[512,1024]{1,0:T(8,128)S(1)} custom-call(s32[2]{0:T(128)S(1)} %pad_add_fusion.place_ref, bf16[4,64,1024]{2,1,0:T(8,128)(2,1)S(1)} %pad_maximum_fusion.own_ref, bf16[4,64,1024]{2,1,0:T(8,128)(2,1)S(1)} %collective-permute-done.5.before_ref, bf16[4,64,1024]{2,1,0:T(8,128)(2,1)} %collective-permute-done.6.after_ref, ...), custom_call_target="tpu_custom_call" | custom-call | tf_op jit(solution)/shard_map/pallas_call | solution.py:125
  91.9 0.9 collective-permute-done.8.came_ref
  92.8 1.4 %shard_map.19 = f32[512,1024]{1,0:T(8,128)} custom-call(f32[512,1024]{1,0:T(8,128)S(1)} %shard_map.18.kept_ref, f32[512,1024]{1,0:T(8,128)S(1)} %collective-permute-done.8.came_ref), custom_call_target="tpu_custom_call" | custom-call | tf_op jit(solution)/shard_map/pallas_call | solution.py:92
  (4 shorter events, 0.0 us)
Async XLA Ops:
  0.0 20.0 %collective-permute-start.1 = (bf16[64,1024]{1,0:T(8,128)(2,1)}, bf16[64,1024]{1,0:T(8,128)(2,1)S(1)}, u32[]{:S(2)}, u32[]{:S(2)}) collective-permute-start(bf16[64,1024]{1,0:T(8,128)(2,1)} %bitcast.6), channel_id=1, source_target_pairs={{0,8},{1,25},{2,10},{3,27},{4,12},{5,29},{6,14},{7,31},{8,16},{9,1... | collective-permute-start | bytes 393224 | tf_op jit(solution)/shard_map/ppermute | solution.py:155
  13.3 7.4 %collective-permute-start = (bf16[64,1024]{1,0:T(8,128)(2,1)}, bf16[64,1024]{1,0:T(8,128)(2,1)S(1)}, u32[]{:S(2)}, u32[]{:S(2)}) collective-permute-start(bf16[64,1024]{1,0:T(8,128)(2,1)} %bitcast.7), channel_id=1, source_target_pairs={{0,0},{1,257},{2,354},{3,99},{4,196},{5,453},{6,38},{7,295},{8,392... | collective-permute-start | bytes 393224 | tf_op jit(solution)/shard_map/ppermute | solution.py:157
  18.1 14.4 %collective-permute-start.3 = (bf16[64,1024]{1,0:T(8,128)(2,1)}, bf16[64,1024]{1,0:T(8,128)(2,1)S(1)}, u32[]{:S(2)}, u32[]{:S(2)}) collective-permute-start(bf16[64,1024]{1,0:T(8,128)(2,1)} %bitcast.8), channel_id=1, source_target_pairs={{0,24},{1,9},{2,26},{3,11},{4,28},{5,13},{6,30},{7,15},{8,0},{9,17... | collective-permute-start | bytes 393224 | tf_op jit(solution)/shard_map/ppermute | solution.py:155
  20.7 17.4 %collective-permute-start.2 = (bf16[64,1024]{1,0:T(8,128)(2,1)S(1)}, bf16[64,1024]{1,0:T(8,128)(2,1)S(1)}, u32[]{:S(2)}, u32[]{:S(2)}) collective-permute-start(bf16[64,1024]{1,0:T(8,128)(2,1)S(1)} %collective-permute-done), channel_id=1, source_target_pairs={{0,0},{1,17},{2,10},{3,27},{4,20},{5,5},{6,30},{7,15},{8,8},{9,25}... | collective-permute-start | bytes 393224 | tf_op jit(solution)/shard_map/ppermute | solution.py:161
  30.6 11.4 %collective-permute-start.4 = (bf16[64,1024]{1,0:T(8,128)(2,1)S(1)}, bf16[64,1024]{1,0:T(8,128)(2,1)S(1)}, u32[]{:S(2)}, u32[]{:S(2)}) collective-permute-start(bf16[64,1024]{1,0:T(8,128)(2,1)S(1)} %collective-permute-done.1), channel_id=1, source_target_pairs={{0,8},{1,25},{2,10},{3,27},{4,12},{5,29},{6,14},{7,31},{8,16},{9,1... | collective-permute-start | bytes 393224 | tf_op jit(solution)/shard_map/ppermute | solution.py:155
  43.6 8.7 %copy-start = (bf16[1,64,1024]{2,1,0:T(8,128)(2,1)S(1)}, bf16[1,64,1024]{2,1,0:T(8,128)(2,1)}, u32[]{:S(2)}) copy-start(bf16[1,64,1024]{2,1,0:T(8,128)(2,1)} %param.1) | copy-start | bytes 393220
  43.6 33.5 %all-to-all-start = ((bf16[16,64,1024]{2,1,0:T(8,128)(2,1)}), bf16[16,64,1024]{2,1,0:T(8,128)(2,1)S(1)}, u32[]{:S(2)}, u32[]{:S(2)}) async-start(bf16[16,64,1024]{2,1,0:T(8,128)(2,1)} %broadcast_in_dim.2), calls=%async_computation | async-start | bytes 4194304 | tf_op jit(solution)/shard_map/all_to_all | solution.py:165
  52.4 10.2 %collective-permute-start.5 = (bf16[4,64,1024]{2,1,0:T(8,128)(2,1)S(1)}, bf16[4,64,1024]{2,1,0:T(8,128)(2,1)S(1)}, u32[]{:S(2)}, u32[]{:S(2)}) collective-permute-start(bf16[4,64,1024]{2,1,0:T(8,128)(2,1)S(1)} %pad_maximum_fusion.own_ref), channel_id=1, source_target_pairs={{0,2},{1,31},{2,4},{3,1},{4,6},{5,3},{6,8},{7,5},{8,10},{9,7},{10,... | collective-permute-start | bytes 1572872 | tf_op jit(solution)/shard_map/ppermute | solution.py:155
  54.4 14.1 %collective-permute-start.6 = (bf16[4,64,1024]{2,1,0:T(8,128)(2,1)S(1)}, bf16[4,64,1024]{2,1,0:T(8,128)(2,1)}, u32[]{:S(2)}, u32[]{:S(2)}) collective-permute-start(bf16[4,64,1024]{2,1,0:T(8,128)(2,1)S(1)} %pad_maximum_fusion.own_ref), channel_id=1, source_target_pairs={{0,30},{1,3},{2,0},{3,5},{4,2},{5,7},{6,4},{7,9},{8,6},{9,11},{10,... | collective-permute-start | bytes 1572872 | tf_op jit(solution)/shard_map/ppermute | solution.py:155
  62.7 13.3 %collective-permute-start.7 = (bf16[4,64,1024]{2,1,0:T(8,128)(2,1)S(1)}, bf16[4,64,1024]{2,1,0:T(8,128)(2,1)}, u32[]{:S(2)}, u32[]{:S(2)}) collective-permute-start(bf16[4,64,1024]{2,1,0:T(8,128)(2,1)S(1)} %collective-permute-done.5.before_ref), channel_id=1, source_target_pairs={{0,2},{1,31},{2,4},{3,1},{4,6},{5,3},{6,8},{7,5},{8,10},{9,7},{10,... | collective-permute-start | bytes 1572872 | tf_op jit(solution)/shard_map/ppermute | solution.py:155
  80.1 12.7 %collective-permute-start.8 = (f32[512,1024]{1,0:T(8,128)S(1)}, f32[512,1024]{1,0:T(8,128)S(1)}, u32[]{:S(2)}, u32[]{:S(2)}) collective-permute-start(f32[512,1024]{1,0:T(8,128)S(1)} %get-tuple-element.20), channel_id=1, source_target_pairs={{0,1},{1,0},{2,3},{3,2},{4,5},{5,4},{6,7},{7,6},{8,9},{9,8},{10,11... | collective-permute-start | bytes 6291464 | tf_op jit(solution)/shard_map/ppermute | solution.py:174

commit v4 on v3

--- a/solution.py
+++ b/solution.py
@@ -166,7 +166,7 @@
 
     held = jnp.stack([own, behind, ahead, across])
     before = along(held, 1)
-    after = along(held, -1)
+    after = along(lax.optimization_barrier((held, before))[0], -1)
     far = along(before, 1)
 
     place = jnp.stack([col, depth])

time: 94.7 us -> 94.6 us (level)
  starting transfers between devices: 57.9 us -> 56.3 us
  waiting for transfers between devices: 27.3 us -> 28.7 us
    ppermute x6, waiting for transfers between devices: 18.9 us -> 21.6 us  [along(): return lax.ppermute(value, axes, hops)]
    ppermute x1, starting transfers between devices: 8.97 us -> 7.39 us  [body(): return finished(kept, lax.ppermute(sent, 'depth', [(0, 1), (1, 0)]))]
    all_to_all x1, waiting for transfers between devices: 1.17 us -> 0.01 us  [body(): raw = lax.all_to_all(copies, 'row', split_axis=0, concat_axis=0, tiled=True)]
  transfers between devices with their start and end apart: 10 -> 10, of which waited for: 8 -> 7; matrix products, arithmetic and copies ran while one was open for 0% -> 0% of each run, Pallas kernels for 3% -> 3%
where the time goes in v4:
time: 94.6 us; the launch traced here: 94.1 us
  starting transfers between devices  56.3 us (60%)
  waiting for transfers between devices  28.7 us (30%)
  Pallas kernels  7.2 us (8%)
  local copies, waits for them, and re-layouts  1.58 us (2%)
    ppermute x6, starting transfers between devices, along(): return lax.ppermute(value, axes, hops)  25.5 us
    ppermute x6, waiting for transfers between devices, along(): return lax.ppermute(value, axes, hops)  21.6 us
    ppermute x1, starting transfers between devices, body(): piece = lax.ppermute(piece, axes, mirror)  9.88 us
    all_to_all x1, starting transfers between devices, body(): raw = lax.all_to_all(copies, 'row', split_axis=0, concat_axis=0, tiled=True)  8.73 us
    ppermute x1, starting transfers between devices, body(): return finished(kept, lax.ppermute(sent, 'depth', [(0, 1), (1, 0)]))  7.39 us
    ppermute x1, waiting for transfers between devices, body(): piece = lax.ppermute(piece, axes, mirror)  5.58 us
    ppermute x1, starting transfers between devices, body(): piece = lax.ppermute(own, axes, spread)  4.82 us
    pallas_call x1, Pallas kernels, partial_products(): pl.pallas_call(send_kernel, out_shape=(product, jax.ShapeDtypeStruct((wid...  2.97 us
  transfers between devices with their start and end apart: 10, of which 7 were waited for; matrix products, arithmetic and copies ran while one was open for 0% of the time, Pallas kernels for 3%

profile of v4, /device:TPU:1, one launch (start us, length us, event | category | flops | bytes accessed | tf_op | source)
XLA Modules:
  0.0 94.1 jit_solution(8544208948183761386)
XLA Ops:
  0.0 13.3 %collective-permute-start.1 = (bf16[64,1024]{1,0:T(8,128)(2,1)}, bf16[64,1024]{1,0:T(8,128)(2,1)S(1)}, u32[]{:S(2)}, u32[]{:S(2)}) collective-permute-start(bf16[64,1024]{1,0:T(8,128)(2,1)} %bitcast.6), channel_id=1, source_target_pairs={{0,8},{1,25},{2,10},{3,27},{4,12},{5,29},{6,14},{7,31},{8,16},{9,1... | collective-permute-start | bytes 393224 | tf_op jit(solution)/shard_map/ppermute | solution.py:155
  13.3 4.8 %collective-permute-start = (bf16[64,1024]{1,0:T(8,128)(2,1)}, bf16[64,1024]{1,0:T(8,128)(2,1)S(1)}, u32[]{:S(2)}, u32[]{:S(2)}) collective-permute-start(bf16[64,1024]{1,0:T(8,128)(2,1)} %bitcast.7), channel_id=1, source_target_pairs={{0,0},{1,257},{2,354},{3,99},{4,196},{5,453},{6,38},{7,295},{8,392... | collective-permute-start | bytes 393224 | tf_op jit(solution)/shard_map/ppermute | solution.py:157
  18.1 1.9 %collective-permute-start.3 = (bf16[64,1024]{1,0:T(8,128)(2,1)}, bf16[64,1024]{1,0:T(8,128)(2,1)S(1)}, u32[]{:S(2)}, u32[]{:S(2)}) collective-permute-start(bf16[64,1024]{1,0:T(8,128)(2,1)} %bitcast.8), channel_id=1, source_target_pairs={{0,24},{1,9},{2,26},{3,11},{4,28},{5,13},{6,30},{7,15},{8,0},{9,17... | collective-permute-start | bytes 393224 | tf_op jit(solution)/shard_map/ppermute | solution.py:155
  20.0 0.0 collective-permute-done.1
  20.1 0.7 collective-permute-done
  20.7 9.9 %collective-permute-start.2 = (bf16[64,1024]{1,0:T(8,128)(2,1)S(1)}, bf16[64,1024]{1,0:T(8,128)(2,1)S(1)}, u32[]{:S(2)}, u32[]{:S(2)}) collective-permute-start(bf16[64,1024]{1,0:T(8,128)(2,1)S(1)} %collective-permute-done), channel_id=1, source_target_pairs={{0,0},{1,17},{2,10},{3,27},{4,20},{5,5},{6,30},{7,15},{8,8},{9,25}... | collective-permute-start | bytes 393224 | tf_op jit(solution)/shard_map/ppermute | solution.py:161
  30.6 1.9 %collective-permute-start.4 = (bf16[64,1024]{1,0:T(8,128)(2,1)S(1)}, bf16[64,1024]{1,0:T(8,128)(2,1)S(1)}, u32[]{:S(2)}, u32[]{:S(2)}) collective-permute-start(bf16[64,1024]{1,0:T(8,128)(2,1)S(1)} %collective-permute-done.1), channel_id=1, source_target_pairs={{0,8},{1,25},{2,10},{3,27},{4,12},{5,29},{6,14},{7,31},{8,16},{9,1... | collective-permute-start | bytes 393224 | tf_op jit(solution)/shard_map/ppermute | solution.py:155
  32.5 5.6 %collective-permute-done.2 = bf16[64,1024]{1,0:T(8,128)(2,1)S(1)} collective-permute-done((bf16[64,1024]{1,0:T(8,128)(2,1)S(1)}, bf16[64,1024]{1,0:T(8,128)(2,1)S(1)}, u32[]{:S(2)}, u32[]{:S(2)}) %collective-permute-start.2) | collective-permute-done | bytes 131104 | tf_op jit(solution)/shard_map/ppermute | solution.py:161
  38.1 3.9 %collective-permute-done.4 = bf16[64,1024]{1,0:T(8,128)(2,1)S(1)} collective-permute-done((bf16[64,1024]{1,0:T(8,128)(2,1)S(1)}, bf16[64,1024]{1,0:T(8,128)(2,1)S(1)}, u32[]{:S(2)}, u32[]{:S(2)}) %collective-permute-start.4) | collective-permute-done | bytes 131104 | tf_op jit(solution)/shard_map/ppermute | solution.py:155
  42.0 1.6 %broadcast_in_dim.2 = bf16[16,64,1024]{2,1,0:T(8,128)(2,1)} broadcast(bf16[64,1024]{1,0:T(8,128)(2,1)S(1)} %collective-permute-done.2), dimensions={1,2} | broadcast | bytes 2228224 | tf_op jit(solution)/shard_map/broadcast_in_dim | solution.py:164
  43.6 8.7 %all-to-all-start = ((bf16[16,64,1024]{2,1,0:T(8,128)(2,1)}), bf16[16,64,1024]{2,1,0:T(8,128)(2,1)S(1)}, u32[]{:S(2)}, u32[]{:S(2)}) async-start(bf16[16,64,1024]{2,1,0:T(8,128)(2,1)} %broadcast_in_dim.2), calls=%async_computation | async-start | bytes 4194304 | tf_op jit(solution)/shard_map/all_to_all | solution.py:165
  52.4 0.1 pad_maximum_fusion.own_ref
  52.4 1.9 %collective-permute-start.5 = (bf16[4,64,1024]{2,1,0:T(8,128)(2,1)S(1)}, bf16[4,64,1024]{2,1,0:T(8,128)(2,1)S(1)}, u32[]{:S(2)}, u32[]{:S(2)}) collective-permute-start(bf16[4,64,1024]{2,1,0:T(8,128)(2,1)S(1)} %pad_maximum_fusion.own_ref), channel_id=1, source_target_pairs={{0,2},{1,31},{2,4},{3,1},{4,6},{5,3},{6,8},{7,5},{8,10},{9,7},{10,... | collective-permute-start | bytes 1572872 | tf_op jit(solution)/shard_map/ppermute | solution.py:155
  54.4 8.3 %collective-permute-done.5.before_ref = bf16[4,64,1024]{2,1,0:T(8,128)(2,1)S(1)} collective-permute-done((bf16[4,64,1024]{2,1,0:T(8,128)(2,1)S(1)}, bf16[4,64,1024]{2,1,0:T(8,128)(2,1)S(1)}, u32[]{:S(2)}, u32[]{:S(2)}) %collective-permute-start.5) | collective-permute-done | bytes 524320 | tf_op jit(solution)/shard_map/ppermute | solution.py:155
  62.7 2.1 %collective-permute-start.6 = (bf16[4,64,1024]{2,1,0:T(8,128)(2,1)S(1)}, bf16[4,64,1024]{2,1,0:T(8,128)(2,1)}, u32[]{:S(2)}, u32[]{:S(2)}) collective-permute-start(bf16[4,64,1024]{2,1,0:T(8,128)(2,1)S(1)} %pad_maximum_fusion.own_ref), channel_id=1, source_target_pairs={{0,30},{1,3},{2,0},{3,5},{4,2},{5,7},{6,4},{7,9},{8,6},{9,11},{10,... | collective-permute-start | bytes 1572872 | tf_op jit(solution)/shard_map/ppermute | solution.py:155
  64.7 4.4 %collective-permute-start.7 = (bf16[4,64,1024]{2,1,0:T(8,128)(2,1)S(1)}, bf16[4,64,1024]{2,1,0:T(8,128)(2,1)}, u32[]{:S(2)}, u32[]{:S(2)}) collective-permute-start(bf16[4,64,1024]{2,1,0:T(8,128)(2,1)S(1)} %collective-permute-done.5.before_ref), channel_id=1, source_target_pairs={{0,2},{1,31},{2,4},{3,1},{4,6},{5,3},{6,8},{7,5},{8,10},{9,7},{10,... | collective-permute-start | bytes 1572872 | tf_op jit(solution)/shard_map/ppermute | solution.py:155
  69.2 0.1 pad_add_fusion.place_ref
  69.2 5.1 %collective-permute-done.6.after_ref = bf16[4,64,1024]{2,1,0:T(8,128)(2,1)} collective-permute-done((bf16[4,64,1024]{2,1,0:T(8,128)(2,1)S(1)}, bf16[4,64,1024]{2,1,0:T(8,128)(2,1)}, u32[]{:S(2)}, u32[]{:S(2)}) %collective-permute-start.6) | collective-permute-done | bytes 524320 | tf_op jit(solution)/shard_map/ppermute | solution.py:155
  74.3 4.3 %collective-permute-done.7.far_ref = bf16[4,64,1024]{2,1,0:T(8,128)(2,1)} collective-permute-done((bf16[4,64,1024]{2,1,0:T(8,128)(2,1)S(1)}, bf16[4,64,1024]{2,1,0:T(8,128)(2,1)}, u32[]{:S(2)}, u32[]{:S(2)}) %collective-permute-start.7) | collective-permute-done | bytes 524320 | tf_op jit(solution)/shard_map/ppermute | solution.py:155
  78.6 3.0 %shard_map.17 = (f32[512,1024]{1,0:T(8,128)S(1)}, bf16[1024,1024]{1,0:T(8,128)(2,1)S(1)}) custom-call(s32[2]{0:T(128)S(1)} %pad_add_fusion.place_ref, bf16[4,64,1024]{2,1,0:T(8,128)(2,1)S(1)} %pad_maximum_fusion.own_ref, bf16[4,64,1024]{2,1,0:T(8,128)(2,1)S(1)} %collective-permute-done.5.before_ref, bf16[4,64,1024]{2,1,0:T(8,128)(2,1)} %collective-permute-done.6.after_ref, ...), custom_call_target="tpu_custom_call" | custom-call | tf_op jit(solution)/shard_map/pallas_call | solution.py:114
  81.6 7.4 %collective-permute-start.8 = (f32[512,1024]{1,0:T(8,128)S(1)}, f32[512,1024]{1,0:T(8,128)S(1)}, u32[]{:S(2)}, u32[]{:S(2)}) collective-permute-start(f32[512,1024]{1,0:T(8,128)S(1)} %get-tuple-element.22), channel_id=1, source_target_pairs={{0,1},{1,0},{2,3},{3,2},{4,5},{5,4},{6,7},{7,6},{8,9},{9,8},{10,11... | collective-permute-start | bytes 6291464 | tf_op jit(solution)/shard_map/ppermute | solution.py:174
  89.0 2.8 %shard_map.18.kept_ref = f32[512,1024]{1,0:T(8,128)S(1)} custom-call(s32[2]{0:T(128)S(1)} %pad_add_fusion.place_ref, bf16[4,64,1024]{2,1,0:T(8,128)(2,1)S(1)} %pad_maximum_fusion.own_ref, bf16[4,64,1024]{2,1,0:T(8,128)(2,1)S(1)} %collective-permute-done.5.before_ref, bf16[4,64,1024]{2,1,0:T(8,128)(2,1)} %collective-permute-done.6.after_ref, ...), custom_call_target="tpu_custom_call" | custom-call | tf_op jit(solution)/shard_map/pallas_call | solution.py:125
  91.8 0.9 collective-permute-done.8.came_ref
  92.7 1.4 %shard_map.19 = f32[512,1024]{1,0:T(8,128)} custom-call(f32[512,1024]{1,0:T(8,128)S(1)} %shard_map.18.kept_ref, f32[512,1024]{1,0:T(8,128)S(1)} %collective-permute-done.8.came_ref), custom_call_target="tpu_custom_call" | custom-call | tf_op jit(solution)/shard_map/pallas_call | solution.py:92
  (4 shorter events, 0.0 us)
Async XLA Ops:
  0.0 20.0 %collective-permute-start.1 = (bf16[64,1024]{1,0:T(8,128)(2,1)}, bf16[64,1024]{1,0:T(8,128)(2,1)S(1)}, u32[]{:S(2)}, u32[]{:S(2)}) collective-permute-start(bf16[64,1024]{1,0:T(8,128)(2,1)} %bitcast.6), channel_id=1, source_target_pairs={{0,8},{1,25},{2,10},{3,27},{4,12},{5,29},{6,14},{7,31},{8,16},{9,1... | collective-permute-start | bytes 393224 | tf_op jit(solution)/shard_map/ppermute | solution.py:155
  13.3 7.4 %collective-permute-start = (bf16[64,1024]{1,0:T(8,128)(2,1)}, bf16[64,1024]{1,0:T(8,128)(2,1)S(1)}, u32[]{:S(2)}, u32[]{:S(2)}) collective-permute-start(bf16[64,1024]{1,0:T(8,128)(2,1)} %bitcast.7), channel_id=1, source_target_pairs={{0,0},{1,257},{2,354},{3,99},{4,196},{5,453},{6,38},{7,295},{8,392... | collective-permute-start | bytes 393224 | tf_op jit(solution)/shard_map/ppermute | solution.py:157
  18.1 14.4 %collective-permute-start.3 = (bf16[64,1024]{1,0:T(8,128)(2,1)}, bf16[64,1024]{1,0:T(8,128)(2,1)S(1)}, u32[]{:S(2)}, u32[]{:S(2)}) collective-permute-start(bf16[64,1024]{1,0:T(8,128)(2,1)} %bitcast.8), channel_id=1, source_target_pairs={{0,24},{1,9},{2,26},{3,11},{4,28},{5,13},{6,30},{7,15},{8,0},{9,17... | collective-permute-start | bytes 393224 | tf_op jit(solution)/shard_map/ppermute | solution.py:155
  20.7 17.4 %collective-permute-start.2 = (bf16[64,1024]{1,0:T(8,128)(2,1)S(1)}, bf16[64,1024]{1,0:T(8,128)(2,1)S(1)}, u32[]{:S(2)}, u32[]{:S(2)}) collective-permute-start(bf16[64,1024]{1,0:T(8,128)(2,1)S(1)} %collective-permute-done), channel_id=1, source_target_pairs={{0,0},{1,17},{2,10},{3,27},{4,20},{5,5},{6,30},{7,15},{8,8},{9,25}... | collective-permute-start | bytes 393224 | tf_op jit(solution)/shard_map/ppermute | solution.py:161
  30.6 11.4 %collective-permute-start.4 = (bf16[64,1024]{1,0:T(8,128)(2,1)S(1)}, bf16[64,1024]{1,0:T(8,128)(2,1)S(1)}, u32[]{:S(2)}, u32[]{:S(2)}) collective-permute-start(bf16[64,1024]{1,0:T(8,128)(2,1)S(1)} %collective-permute-done.1), channel_id=1, source_target_pairs={{0,8},{1,25},{2,10},{3,27},{4,12},{5,29},{6,14},{7,31},{8,16},{9,1... | collective-permute-start | bytes 393224 | tf_op jit(solution)/shard_map/ppermute | solution.py:155
  43.6 8.7 %copy-start = (bf16[1,64,1024]{2,1,0:T(8,128)(2,1)S(1)}, bf16[1,64,1024]{2,1,0:T(8,128)(2,1)}, u32[]{:S(2)}) copy-start(bf16[1,64,1024]{2,1,0:T(8,128)(2,1)} %param.1) | copy-start | bytes 393220
  43.6 35.0 %all-to-all-start = ((bf16[16,64,1024]{2,1,0:T(8,128)(2,1)}), bf16[16,64,1024]{2,1,0:T(8,128)(2,1)S(1)}, u32[]{:S(2)}, u32[]{:S(2)}) async-start(bf16[16,64,1024]{2,1,0:T(8,128)(2,1)} %broadcast_in_dim.2), calls=%async_computation | async-start | bytes 4194304 | tf_op jit(solution)/shard_map/all_to_all | solution.py:165
  52.4 10.2 %collective-permute-start.5 = (bf16[4,64,1024]{2,1,0:T(8,128)(2,1)S(1)}, bf16[4,64,1024]{2,1,0:T(8,128)(2,1)S(1)}, u32[]{:S(2)}, u32[]{:S(2)}) collective-permute-start(bf16[4,64,1024]{2,1,0:T(8,128)(2,1)S(1)} %pad_maximum_fusion.own_ref), channel_id=1, source_target_pairs={{0,2},{1,31},{2,4},{3,1},{4,6},{5,3},{6,8},{7,5},{8,10},{9,7},{10,... | collective-permute-start | bytes 1572872 | tf_op jit(solution)/shard_map/ppermute | solution.py:155
  62.7 11.7 %collective-permute-start.6 = (bf16[4,64,1024]{2,1,0:T(8,128)(2,1)S(1)}, bf16[4,64,1024]{2,1,0:T(8,128)(2,1)}, u32[]{:S(2)}, u32[]{:S(2)}) collective-permute-start(bf16[4,64,1024]{2,1,0:T(8,128)(2,1)S(1)} %pad_maximum_fusion.own_ref), channel_id=1, source_target_pairs={{0,30},{1,3},{2,0},{3,5},{4,2},{5,7},{6,4},{7,9},{8,6},{9,11},{10,... | collective-permute-start | bytes 1572872 | tf_op jit(solution)/shard_map/ppermute | solution.py:155
  64.7 13.9 %collective-permute-start.7 = (bf16[4,64,1024]{2,1,0:T(8,128)(2,1)S(1)}, bf16[4,64,1024]{2,1,0:T(8,128)(2,1)}, u32[]{:S(2)}, u32[]{:S(2)}) collective-permute-start(bf16[4,64,1024]{2,1,0:T(8,128)(2,1)S(1)} %collective-permute-done.5.before_ref), channel_id=1, source_target_pairs={{0,2},{1,31},{2,4},{3,1},{4,6},{5,3},{6,8},{7,5},{8,10},{9,7},{10,... | collective-permute-start | bytes 1572872 | tf_op jit(solution)/shard_map/ppermute | solution.py:155
  81.6 11.2 %collective-permute-start.8 = (f32[512,1024]{1,0:T(8,128)S(1)}, f32[512,1024]{1,0:T(8,128)S(1)}, u32[]{:S(2)}, u32[]{:S(2)}) collective-permute-start(f32[512,1024]{1,0:T(8,128)S(1)} %get-tuple-element.22), channel_id=1, source_target_pairs={{0,1},{1,0},{2,3},{3,2},{4,5},{5,4},{6,7},{7,6},{8,9},{9,8},{10,11... | collective-permute-start | bytes 6291464 | tf_op jit(solution)/shard_map/ppermute | solution.py:174

commit v5 on v4

--- a/solution.py
+++ b/solution.py
@@ -6,7 +6,7 @@
 from jax.sharding import PartitionSpec as P
 
 STRIDE = 4
-CHUNKS = 4
+CHUNKS = 2
 TURN = 5
 
 

time: 94.6 us -> 94.6 us (level)
  no operation moved by 1% of the time
where the time goes in v5:
time: 94.6 us; the launch traced here: 94.1 us
  starting transfers between devices  56.3 us (60%)
  waiting for transfers between devices  28.7 us (30%)
  Pallas kernels  7.2 us (8%)
  local copies, waits for them, and re-layouts  1.58 us (2%)
    ppermute x6, starting transfers between devices, along(): return lax.ppermute(value, axes, hops)  25.5 us
    ppermute x6, waiting for transfers between devices, along(): return lax.ppermute(value, axes, hops)  21.6 us
    ppermute x1, starting transfers between devices, body(): piece = lax.ppermute(piece, axes, mirror)  9.88 us
    all_to_all x1, starting transfers between devices, body(): raw = lax.all_to_all(copies, 'row', split_axis=0, concat_axis=0, tiled=True)  8.73 us
    ppermute x1, starting transfers between devices, body(): return finished(kept, lax.ppermute(sent, 'depth', [(0, 1), (1, 0)]))  7.39 us
    ppermute x1, waiting for transfers between devices, body(): piece = lax.ppermute(piece, axes, mirror)  5.58 us
    ppermute x1, starting transfers between devices, body(): piece = lax.ppermute(own, axes, spread)  4.82 us
    pallas_call x1, Pallas kernels, partial_products(): pl.pallas_call(send_kernel, out_shape=(product, jax.ShapeDtypeStruct((wid...  2.97 us
  transfers between devices with their start and end apart: 10, of which 7 were waited for; matrix products, arithmetic and copies ran while one was open for 0% of the time, Pallas kernels for 3%

profile of v5, /device:TPU:1, one launch (start us, length us, event | category | flops | bytes accessed | tf_op | source)
XLA Modules:
  0.0 94.1 jit_solution(4307393175001034506)
XLA Ops:
  0.0 13.3 %collective-permute-start.1 = (bf16[64,1024]{1,0:T(8,128)(2,1)}, bf16[64,1024]{1,0:T(8,128)(2,1)S(1)}, u32[]{:S(2)}, u32[]{:S(2)}) collective-permute-start(bf16[64,1024]{1,0:T(8,128)(2,1)} %bitcast.6), channel_id=1, source_target_pairs={{0,8},{1,25},{2,10},{3,27},{4,12},{5,29},{6,14},{7,31},{8,16},{9,1... | collective-permute-start | bytes 393224 | tf_op jit(solution)/shard_map/ppermute | solution.py:155
  13.3 4.8 %collective-permute-start = (bf16[64,1024]{1,0:T(8,128)(2,1)}, bf16[64,1024]{1,0:T(8,128)(2,1)S(1)}, u32[]{:S(2)}, u32[]{:S(2)}) collective-permute-start(bf16[64,1024]{1,0:T(8,128)(2,1)} %bitcast.7), channel_id=1, source_target_pairs={{0,0},{1,257},{2,354},{3,99},{4,196},{5,453},{6,38},{7,295},{8,392... | collective-permute-start | bytes 393224 | tf_op jit(solution)/shard_map/ppermute | solution.py:157
  18.1 1.9 %collective-permute-start.3 = (bf16[64,1024]{1,0:T(8,128)(2,1)}, bf16[64,1024]{1,0:T(8,128)(2,1)S(1)}, u32[]{:S(2)}, u32[]{:S(2)}) collective-permute-start(bf16[64,1024]{1,0:T(8,128)(2,1)} %bitcast.8), channel_id=1, source_target_pairs={{0,24},{1,9},{2,26},{3,11},{4,28},{5,13},{6,30},{7,15},{8,0},{9,17... | collective-permute-start | bytes 393224 | tf_op jit(solution)/shard_map/ppermute | solution.py:155
  20.0 0.0 collective-permute-done.1
  20.1 0.7 collective-permute-done
  20.7 9.9 %collective-permute-start.2 = (bf16[64,1024]{1,0:T(8,128)(2,1)S(1)}, bf16[64,1024]{1,0:T(8,128)(2,1)S(1)}, u32[]{:S(2)}, u32[]{:S(2)}) collective-permute-start(bf16[64,1024]{1,0:T(8,128)(2,1)S(1)} %collective-permute-done), channel_id=1, source_target_pairs={{0,0},{1,17},{2,10},{3,27},{4,20},{5,5},{6,30},{7,15},{8,8},{9,25}... | collective-permute-start | bytes 393224 | tf_op jit(solution)/shard_map/ppermute | solution.py:161
  30.6 1.9 %collective-permute-start.4 = (bf16[64,1024]{1,0:T(8,128)(2,1)S(1)}, bf16[64,1024]{1,0:T(8,128)(2,1)S(1)}, u32[]{:S(2)}, u32[]{:S(2)}) collective-permute-start(bf16[64,1024]{1,0:T(8,128)(2,1)S(1)} %collective-permute-done.1), channel_id=1, source_target_pairs={{0,8},{1,25},{2,10},{3,27},{4,12},{5,29},{6,14},{7,31},{8,16},{9,1... | collective-permute-start | bytes 393224 | tf_op jit(solution)/shard_map/ppermute | solution.py:155
  32.5 5.6 %collective-permute-done.2 = bf16[64,1024]{1,0:T(8,128)(2,1)S(1)} collective-permute-done((bf16[64,1024]{1,0:T(8,128)(2,1)S(1)}, bf16[64,1024]{1,0:T(8,128)(2,1)S(1)}, u32[]{:S(2)}, u32[]{:S(2)}) %collective-permute-start.2) | collective-permute-done | bytes 131104 | tf_op jit(solution)/shard_map/ppermute | solution.py:161
  38.1 3.9 %collective-permute-done.4 = bf16[64,1024]{1,0:T(8,128)(2,1)S(1)} collective-permute-done((bf16[64,1024]{1,0:T(8,128)(2,1)S(1)}, bf16[64,1024]{1,0:T(8,128)(2,1)S(1)}, u32[]{:S(2)}, u32[]{:S(2)}) %collective-permute-start.4) | collective-permute-done | bytes 131104 | tf_op jit(solution)/shard_map/ppermute | solution.py:155
  42.0 1.6 %broadcast_in_dim.2 = bf16[16,64,1024]{2,1,0:T(8,128)(2,1)} broadcast(bf16[64,1024]{1,0:T(8,128)(2,1)S(1)} %collective-permute-done.2), dimensions={1,2} | broadcast | bytes 2228224 | tf_op jit(solution)/shard_map/broadcast_in_dim | solution.py:164
  43.6 8.7 %all-to-all-start = ((bf16[16,64,1024]{2,1,0:T(8,128)(2,1)}), bf16[16,64,1024]{2,1,0:T(8,128)(2,1)S(1)}, u32[]{:S(2)}, u32[]{:S(2)}) async-start(bf16[16,64,1024]{2,1,0:T(8,128)(2,1)} %broadcast_in_dim.2), calls=%async_computation | async-start | bytes 4194304 | tf_op jit(solution)/shard_map/all_to_all | solution.py:165
  52.4 0.1 pad_maximum_fusion.own_ref
  52.4 1.9 %collective-permute-start.5 = (bf16[4,64,1024]{2,1,0:T(8,128)(2,1)S(1)}, bf16[4,64,1024]{2,1,0:T(8,128)(2,1)S(1)}, u32[]{:S(2)}, u32[]{:S(2)}) collective-permute-start(bf16[4,64,1024]{2,1,0:T(8,128)(2,1)S(1)} %pad_maximum_fusion.own_ref), channel_id=1, source_target_pairs={{0,2},{1,31},{2,4},{3,1},{4,6},{5,3},{6,8},{7,5},{8,10},{9,7},{10,... | collective-permute-start | bytes 1572872 | tf_op jit(solution)/shard_map/ppermute | solution.py:155
  54.4 8.3 %collective-permute-done.5.before_ref = bf16[4,64,1024]{2,1,0:T(8,128)(2,1)S(1)} collective-permute-done((bf16[4,64,1024]{2,1,0:T(8,128)(2,1)S(1)}, bf16[4,64,1024]{2,1,0:T(8,128)(2,1)S(1)}, u32[]{:S(2)}, u32[]{:S(2)}) %collective-permute-start.5) | collective-permute-done | bytes 524320 | tf_op jit(solution)/shard_map/ppermute | solution.py:155
  62.7 2.1 %collective-permute-start.6 = (bf16[4,64,1024]{2,1,0:T(8,128)(2,1)S(1)}, bf16[4,64,1024]{2,1,0:T(8,128)(2,1)}, u32[]{:S(2)}, u32[]{:S(2)}) collective-permute-start(bf16[4,64,1024]{2,1,0:T(8,128)(2,1)S(1)} %pad_maximum_fusion.own_ref), channel_id=1, source_target_pairs={{0,30},{1,3},{2,0},{3,5},{4,2},{5,7},{6,4},{7,9},{8,6},{9,11},{10,... | collective-permute-start | bytes 1572872 | tf_op jit(solution)/shard_map/ppermute | solution.py:155
  64.7 4.4 %collective-permute-start.7 = (bf16[4,64,1024]{2,1,0:T(8,128)(2,1)S(1)}, bf16[4,64,1024]{2,1,0:T(8,128)(2,1)}, u32[]{:S(2)}, u32[]{:S(2)}) collective-permute-start(bf16[4,64,1024]{2,1,0:T(8,128)(2,1)S(1)} %collective-permute-done.5.before_ref), channel_id=1, source_target_pairs={{0,2},{1,31},{2,4},{3,1},{4,6},{5,3},{6,8},{7,5},{8,10},{9,7},{10,... | collective-permute-start | bytes 1572872 | tf_op jit(solution)/shard_map/ppermute | solution.py:155
  69.2 0.1 pad_add_fusion.place_ref
  69.2 5.1 %collective-permute-done.6.after_ref = bf16[4,64,1024]{2,1,0:T(8,128)(2,1)} collective-permute-done((bf16[4,64,1024]{2,1,0:T(8,128)(2,1)S(1)}, bf16[4,64,1024]{2,1,0:T(8,128)(2,1)}, u32[]{:S(2)}, u32[]{:S(2)}) %collective-permute-start.6) | collective-permute-done | bytes 524320 | tf_op jit(solution)/shard_map/ppermute | solution.py:155
  74.3 4.3 %collective-permute-done.7.far_ref = bf16[4,64,1024]{2,1,0:T(8,128)(2,1)} collective-permute-done((bf16[4,64,1024]{2,1,0:T(8,128)(2,1)S(1)}, bf16[4,64,1024]{2,1,0:T(8,128)(2,1)}, u32[]{:S(2)}, u32[]{:S(2)}) %collective-permute-start.7) | collective-permute-done | bytes 524320 | tf_op jit(solution)/shard_map/ppermute | solution.py:155
  78.6 3.0 %shard_map.17 = (f32[512,1024]{1,0:T(8,128)S(1)}, bf16[1024,1024]{1,0:T(8,128)(2,1)S(1)}) custom-call(s32[2]{0:T(128)S(1)} %pad_add_fusion.place_ref, bf16[4,64,1024]{2,1,0:T(8,128)(2,1)S(1)} %pad_maximum_fusion.own_ref, bf16[4,64,1024]{2,1,0:T(8,128)(2,1)S(1)} %collective-permute-done.5.before_ref, bf16[4,64,1024]{2,1,0:T(8,128)(2,1)} %collective-permute-done.6.after_ref, ...), custom_call_target="tpu_custom_call" | custom-call | tf_op jit(solution)/shard_map/pallas_call | solution.py:114
  81.6 7.4 %collective-permute-start.8 = (f32[512,1024]{1,0:T(8,128)S(1)}, f32[512,1024]{1,0:T(8,128)S(1)}, u32[]{:S(2)}, u32[]{:S(2)}) collective-permute-start(f32[512,1024]{1,0:T(8,128)S(1)} %get-tuple-element.22), channel_id=1, source_target_pairs={{0,1},{1,0},{2,3},{3,2},{4,5},{5,4},{6,7},{7,6},{8,9},{9,8},{10,11... | collective-permute-start | bytes 6291464 | tf_op jit(solution)/shard_map/ppermute | solution.py:174
  89.0 2.8 %shard_map.18.kept_ref = f32[512,1024]{1,0:T(8,128)S(1)} custom-call(s32[2]{0:T(128)S(1)} %pad_add_fusion.place_ref, bf16[4,64,1024]{2,1,0:T(8,128)(2,1)S(1)} %pad_maximum_fusion.own_ref, bf16[4,64,1024]{2,1,0:T(8,128)(2,1)S(1)} %collective-permute-done.5.before_ref, bf16[4,64,1024]{2,1,0:T(8,128)(2,1)} %collective-permute-done.6.after_ref, ...), custom_call_target="tpu_custom_call" | custom-call | tf_op jit(solution)/shard_map/pallas_call | solution.py:125
  91.8 0.9 collective-permute-done.8.came_ref
  92.7 1.4 %shard_map.19 = f32[512,1024]{1,0:T(8,128)} custom-call(f32[512,1024]{1,0:T(8,128)S(1)} %shard_map.18.kept_ref, f32[512,1024]{1,0:T(8,128)S(1)} %collective-permute-done.8.came_ref), custom_call_target="tpu_custom_call" | custom-call | tf_op jit(solution)/shard_map/pallas_call | solution.py:92
  (4 shorter events, 0.0 us)
Async XLA Ops:
  0.0 20.0 %collective-permute-start.1 = (bf16[64,1024]{1,0:T(8,128)(2,1)}, bf16[64,1024]{1,0:T(8,128)(2,1)S(1)}, u32[]{:S(2)}, u32[]{:S(2)}) collective-permute-start(bf16[64,1024]{1,0:T(8,128)(2,1)} %bitcast.6), channel_id=1, source_target_pairs={{0,8},{1,25},{2,10},{3,27},{4,12},{5,29},{6,14},{7,31},{8,16},{9,1... | collective-permute-start | bytes 393224 | tf_op jit(solution)/shard_map/ppermute | solution.py:155
  13.3 7.4 %collective-permute-start = (bf16[64,1024]{1,0:T(8,128)(2,1)}, bf16[64,1024]{1,0:T(8,128)(2,1)S(1)}, u32[]{:S(2)}, u32[]{:S(2)}) collective-permute-start(bf16[64,1024]{1,0:T(8,128)(2,1)} %bitcast.7), channel_id=1, source_target_pairs={{0,0},{1,257},{2,354},{3,99},{4,196},{5,453},{6,38},{7,295},{8,392... | collective-permute-start | bytes 393224 | tf_op jit(solution)/shard_map/ppermute | solution.py:157
  18.1 14.4 %collective-permute-start.3 = (bf16[64,1024]{1,0:T(8,128)(2,1)}, bf16[64,1024]{1,0:T(8,128)(2,1)S(1)}, u32[]{:S(2)}, u32[]{:S(2)}) collective-permute-start(bf16[64,1024]{1,0:T(8,128)(2,1)} %bitcast.8), channel_id=1, source_target_pairs={{0,24},{1,9},{2,26},{3,11},{4,28},{5,13},{6,30},{7,15},{8,0},{9,17... | collective-permute-start | bytes 393224 | tf_op jit(solution)/shard_map/ppermute | solution.py:155
  20.7 17.4 %collective-permute-start.2 = (bf16[64,1024]{1,0:T(8,128)(2,1)S(1)}, bf16[64,1024]{1,0:T(8,128)(2,1)S(1)}, u32[]{:S(2)}, u32[]{:S(2)}) collective-permute-start(bf16[64,1024]{1,0:T(8,128)(2,1)S(1)} %collective-permute-done), channel_id=1, source_target_pairs={{0,0},{1,17},{2,10},{3,27},{4,20},{5,5},{6,30},{7,15},{8,8},{9,25}... | collective-permute-start | bytes 393224 | tf_op jit(solution)/shard_map/ppermute | solution.py:161
  30.6 11.4 %collective-permute-start.4 = (bf16[64,1024]{1,0:T(8,128)(2,1)S(1)}, bf16[64,1024]{1,0:T(8,128)(2,1)S(1)}, u32[]{:S(2)}, u32[]{:S(2)}) collective-permute-start(bf16[64,1024]{1,0:T(8,128)(2,1)S(1)} %collective-permute-done.1), channel_id=1, source_target_pairs={{0,8},{1,25},{2,10},{3,27},{4,12},{5,29},{6,14},{7,31},{8,16},{9,1... | collective-permute-start | bytes 393224 | tf_op jit(solution)/shard_map/ppermute | solution.py:155
  43.6 8.7 %copy-start = (bf16[1,64,1024]{2,1,0:T(8,128)(2,1)S(1)}, bf16[1,64,1024]{2,1,0:T(8,128)(2,1)}, u32[]{:S(2)}) copy-start(bf16[1,64,1024]{2,1,0:T(8,128)(2,1)} %param.1) | copy-start | bytes 393220
  43.6 35.0 %all-to-all-start = ((bf16[16,64,1024]{2,1,0:T(8,128)(2,1)}), bf16[16,64,1024]{2,1,0:T(8,128)(2,1)S(1)}, u32[]{:S(2)}, u32[]{:S(2)}) async-start(bf16[16,64,1024]{2,1,0:T(8,128)(2,1)} %broadcast_in_dim.2), calls=%async_computation | async-start | bytes 4194304 | tf_op jit(solution)/shard_map/all_to_all | solution.py:165
  52.4 10.2 %collective-permute-start.5 = (bf16[4,64,1024]{2,1,0:T(8,128)(2,1)S(1)}, bf16[4,64,1024]{2,1,0:T(8,128)(2,1)S(1)}, u32[]{:S(2)}, u32[]{:S(2)}) collective-permute-start(bf16[4,64,1024]{2,1,0:T(8,128)(2,1)S(1)} %pad_maximum_fusion.own_ref), channel_id=1, source_target_pairs={{0,2},{1,31},{2,4},{3,1},{4,6},{5,3},{6,8},{7,5},{8,10},{9,7},{10,... | collective-permute-start | bytes 1572872 | tf_op jit(solution)/shard_map/ppermute | solution.py:155
  62.7 11.7 %collective-permute-start.6 = (bf16[4,64,1024]{2,1,0:T(8,128)(2,1)S(1)}, bf16[4,64,1024]{2,1,0:T(8,128)(2,1)}, u32[]{:S(2)}, u32[]{:S(2)}) collective-permute-start(bf16[4,64,1024]{2,1,0:T(8,128)(2,1)S(1)} %pad_maximum_fusion.own_ref), channel_id=1, source_target_pairs={{0,30},{1,3},{2,0},{3,5},{4,2},{5,7},{6,4},{7,9},{8,6},{9,11},{10,... | collective-permute-start | bytes 1572872 | tf_op jit(solution)/shard_map/ppermute | solution.py:155
  64.7 13.9 %collective-permute-start.7 = (bf16[4,64,1024]{2,1,0:T(8,128)(2,1)S(1)}, bf16[4,64,1024]{2,1,0:T(8,128)(2,1)}, u32[]{:S(2)}, u32[]{:S(2)}) collective-permute-start(bf16[4,64,1024]{2,1,0:T(8,128)(2,1)S(1)} %collective-permute-done.5.before_ref), channel_id=1, source_target_pairs={{0,2},{1,31},{2,4},{3,1},{4,6},{5,3},{6,8},{7,5},{8,10},{9,7},{10,... | collective-permute-start | bytes 1572872 | tf_op jit(solution)/shard_map/ppermute | solution.py:155
  81.6 11.2 %collective-permute-start.8 = (f32[512,1024]{1,0:T(8,128)S(1)}, f32[512,1024]{1,0:T(8,128)S(1)}, u32[]{:S(2)}, u32[]{:S(2)}) collective-permute-start(f32[512,1024]{1,0:T(8,128)S(1)} %get-tuple-element.22), channel_id=1, source_target_pairs={{0,1},{1,0},{2,3},{3,2},{4,5},{5,4},{6,7},{7,6},{8,9},{9,8},{10,11... | collective-permute-start | bytes 6291464 | tf_op jit(solution)/shard_map/ppermute | solution.py:174
